TPU v7x, 256 devices: a whole 4x4x8 slice. The times are simulated.
256 devices in a mesh: wide: 64 (over x, z, core), narrow: 4 (over y).
Axes of the slice: x: 4, y: 4, z: 8, core: 2. Of those that a mesh axis runs over, the one named last changes fastest.
Arguments:
- block: float32 [4, 8192, 512], P(None, 'wide', 'narrow'), may hold values from -6 to 6
- east_weight: float32 [8192, 512], P('wide', 'narrow'), may hold values from 0.2 to 5
- north_weight: float32 [8192, 512], P('wide', 'narrow'), may hold values from 0.2 to 5
- fine_groups: int32 [8192, 512], P('wide', 'narrow'), may hold values from 0 to 2047
- tiles_one: float32 [4096, 4, 128, 128], P(('wide', 'narrow')), as said below
- columns_one: int32 [4096, 3], P(('wide', 'narrow')), may hold values from 0 to 79
- live_one: int32 [4096, 3], P(('wide', 'narrow')), may hold values 0 or 1
- coarse_groups: int32 [524288], P(('wide', 'narrow')), may hold values from 0 to 255
- tiles_two: float32 [1024, 4, 64, 64], P(('wide', 'narrow')), as said below
- columns_two: int32 [1024, 3], P(('wide', 'narrow')), may hold values from 0 to 19
- live_two: int32 [1024, 3], P(('wide', 'narrow')), may hold values 0 or 1
- coarser_groups: int32 [65536], P(('wide', 'narrow')), may hold values from 0 to 31
- chain_forward: float32 [64, 128, 128], P('wide')
- chain_gain: float32 [64, 128, 128], P('wide')
- chain_backward: float32 [64, 128, 128], P('wide')
Outputs:
- corrected: float32 [4, 8192, 512], P(None, 'wide', 'narrow')
Inputs may be any that keep to these rules, and one draw needn't show every extreme that they name: `tiles_one`: in every row tile, slot 0 is the tile of that row tile with itself, and its diagonal entries lie in 1 to 2. `tiles_two`: in every row tile, slot 0 is the tile of that row tile with itself, and its diagonal entries lie in 1 to 2.
All inputs are finite; a program needn't handle non-finite values. No bound on the sum of `live_one` or of `live_two` on one device may be relied on, other than what follows from the above.
Results may differ from a plain program's by a relative error of at most 0.0001.
Values sent between devices are 32-bit elements; how exact they have to be, the bound alone decides.
A program may use at most 128 MiB of HBM per device.

v0:
```python
import jax
import jax.numpy as jnp
from jax import lax
from jax.sharding import Mesh
from jax.sharding import PartitionSpec as P

COLS = 4
C1 = 2048
C2 = 256
C3L = 32
WIDE = ("wide_0", "wide_1", "wide_2")
WIDE_NARROW = ("wide_0", "wide_1", "wide_2", "narrow")


shift_value = 0.1
jacobi_weight = 0.6
smooth_weight = 0.5


def sent_to_all(shard, axis):
    peers = lax.axis_size(axis)
    return lax.all_to_all(
        jnp.broadcast_to(shard[None], (peers, *shard.shape)), axis, 0, 0, tiled=True
    )


def laid_out(parts, dim):
    dims = list(parts.shape[1:])
    dims[dim] *= parts.shape[0]
    return jnp.moveaxis(parts, 0, dim).reshape(dims)


def gather_directly(shard, axis, dim):
    parts = sent_to_all(shard, axis)
    return laid_out(parts, dim)


def shifted(block, axis, distance):
    devices = range(lax.axis_size(axis))
    route = [(i - distance, i) for i in devices if i - distance in devices]
    return lax.ppermute(block, axis, route)


def with_halo(shard, sides, width):
    edges = {}
    for axis, dim in sides:
        peers, length = (lax.axis_size(axis), shard.shape[dim])
        up = [(i, (i + 1) % peers) for i in range(peers - 1)]
        last = lax.slice_in_dim(shard, length - width, length, axis=dim)
        leading = lax.slice_in_dim(shard, 0, width, axis=dim)
        edges[dim] = (
            lax.ppermute(last, axis, up),
            lax.ppermute(leading, axis, [(b, a) for a, b in up]),
        )
    done = []
    for _, dim in sides:
        low, high = edges[dim]
        around = [(width, width) if d in done else (0, 0) for d in range(shard.ndim)]
        shard = jnp.concatenate([jnp.pad(low, around), shard, jnp.pad(high, around)], axis=dim)
        done.append(dim)
    return shard


def nothing_yet(shard, identity):
    return jax.tree.map(
        lambda a, e: jnp.broadcast_to(jnp.asarray(e, a.dtype), a.shape), shard, identity
    )


def gathered_once(shard, axis):
    leaves = jax.tree.leaves(shard)
    order = sorted(range(len(leaves)), key=lambda k: -leaves[k].size)
    width = (1, *leaves[order[0]].shape)[-1]
    lines = [
        jnp.pad(leaves[k].reshape(-1), (0, -leaves[k].size % width)).reshape(-1, width)
        for k in order
    ]
    both, at, found = (lax.all_gather(jnp.concatenate(lines), axis), 0, {})
    for k, line in zip(order, lines):
        share = both[:, at : at + len(line)].reshape(len(both), -1)
        found[k] = share[:, : leaves[k].size].reshape(-1, *leaves[k].shape)
        at += len(line)
    numbers = iter(range(len(leaves)))
    return jax.tree.map(lambda _: found[next(numbers)], shard)


def gathered_by_type(shard, axis):
    leaves, found = (jax.tree.leaves(shard), {})
    for leading, a in enumerate(leaves):
        if leading not in found:
            alike = [k for k, b in enumerate(leaves) if b.dtype == a.dtype]
            got = (
                gathered_once([leaves[k] for k in alike], axis)
                if len(alike) > 1
                else [lax.all_gather(a, axis)]
            )
            for k, b in zip(alike, got):
                found[k] = b
    numbers = iter(range(len(leaves)))
    return jax.tree.map(lambda _: found[next(numbers)], shard)


def entering(shard, axes, combine, identity, reverse):
    before = start = nothing_yet(shard, identity)
    so_far = shard
    for axis in reversed(axes):
        peers, position = (lax.axis_size(axis), lax.axis_index(axis))
        pieces = gathered_by_type(so_far, axis)
        inside, so_far = (start, start)
        for k in reversed(range(peers)) if reverse else range(peers):
            passed = k > position if reverse else k < position
            so_far = combine(so_far, jax.tree.map(lambda part: part[k], pieces))
            inside = jax.tree.map(lambda new, old: jnp.where(passed, new, old), so_far, inside)
        before = combine(inside, before)
    return before


def combine_fine(field, padded, east_live, west_live, north_live, south_live):
    east_side = padded[:, 2:, 1:-1]
    west_side = padded[:, :-2, 1:-1]
    north_side = padded[:, 1:-1, 2:]
    south_side = padded[:, 1:-1, :-2]
    result = shift_value * field + east_live * (field - east_side) + west_live * (field - west_side)
    return result + north_live * (field - north_side) + south_live * (field - south_side)


def tile_product(tiles, blocks, picked):
    own_part = jnp.einsum("rab,crb->cra", tiles[:, 0], blocks, precision=lax.Precision.HIGHEST)
    other_part = jnp.einsum("rkab,crkb->cra", tiles[:, 1:], picked, precision=lax.Precision.HIGHEST)
    return (own_part + other_part).reshape(blocks.shape[0], -1)


def neighbours(field):
    grouped = gather_directly(field[None], "narrow", 0)
    padded = jnp.pad(grouped, ((1, 1), (0, 0), (0, 0)))
    narrow_pos = lax.axis_index("narrow")
    south_side = lax.dynamic_index_in_dim(padded, narrow_pos, 0, keepdims=False)
    north_side = lax.dynamic_index_in_dim(padded, narrow_pos + 2, 0, keepdims=False)
    west_side = shifted(field, WIDE, 1)
    east_side = shifted(field, WIDE, -1)
    return jnp.stack([field, west_side, east_side, south_side, north_side], axis=1)


def coarse_apply(field, tiles, columns, live):
    tile_count = tiles.shape[0]
    tile_size = tiles.shape[2]
    beside_all = neighbours(field).reshape(COLS, 5 * tile_count, tile_size)
    blocks = field.reshape(COLS, tile_count, tile_size)
    picked = jnp.take(beside_all, columns.reshape(-1), axis=1)
    picked = picked.reshape(COLS, tile_count, columns.shape[1], tile_size)
    picked = picked * (live == 1).astype(jnp.float32)[None, :, :, None]
    return tile_product(tiles, blocks, picked)


def segment_total(values, indices, segment_count):
    return jax.ops.segment_sum(values.T, indices, num_segments=segment_count).T


def smooth_cycle(level, right, levels, coarsest):
    if level == len(levels):
        return coarsest(right)
    apply_op, diagonal, restrict_op, prolong_op = levels[level]
    first_iter = jacobi_weight * right / diagonal
    second_iter = first_iter + jacobi_weight * (right - apply_op(first_iter)) / diagonal
    leftover = right - apply_op(second_iter)
    scaled = leftover / diagonal
    coarse_right = restrict_op(leftover - smooth_weight * apply_op(scaled))
    coarse_answer = smooth_cycle(level + 1, coarse_right, levels, coarsest)
    spread = prolong_op(coarse_answer)
    third_iter = second_iter + (spread - smooth_weight * apply_op(spread) / diagonal)
    fourth_iter = third_iter + jacobi_weight * (right - apply_op(third_iter)) / diagonal
    return fourth_iter + jacobi_weight * (right - apply_op(fourth_iter)) / diagonal


def compose(earlier, later):
    joined = jnp.dot(later[0], earlier[0], precision=lax.Precision.HIGHEST)
    offset = jnp.dot(later[0], earlier[1], precision=lax.Precision.HIGHEST) + later[1]
    return (joined, offset)


def body(
    block,
    east_weight,
    north_weight,
    fine_groups,
    tiles_one,
    columns_one,
    live_one,
    coarse_groups,
    tiles_two,
    columns_two,
    live_two,
    coarser_groups,
    chain_forward,
    chain_gain,
    chain_backward,
):
    rows_local = east_weight.shape[0]
    columns_local = east_weight.shape[1]
    row_global = lax.axis_index(WIDE) * rows_local + lax.broadcasted_iota(
        jnp.int32, east_weight.shape, 0
    )
    column_global = lax.axis_index("narrow") * columns_local + lax.broadcasted_iota(
        jnp.int32, east_weight.shape, 1
    )
    east_live = jnp.where(row_global < rows_local * lax.axis_size(WIDE) - 1, east_weight, 0.0)
    north_live = jnp.where(
        column_global < columns_local * lax.axis_size("narrow") - 1, north_weight, 0.0
    )
    west_edge = shifted(east_live[-1:, :], WIDE, 1)
    west_live = jnp.concatenate([west_edge, east_live[:-1]], axis=0)
    south_edge = shifted(north_live[:, -1:], "narrow", 1)
    south_live = jnp.concatenate([south_edge, north_live[:, :-1]], axis=1)
    fine_diagonal = shift_value + east_live + west_live + north_live + south_live
    fine_ids = fine_groups.reshape(-1)

    def apply_fine(field):
        padded = with_halo(field, ((WIDE, 1), ("narrow", 2)), 1)
        return combine_fine(field, padded, east_live, west_live, north_live, south_live)

    def restrict_fine(field):
        return segment_total(field.reshape(COLS, -1), fine_ids, C1)

    def prolong_fine(coarse):
        return jnp.take(coarse, fine_ids, axis=1).reshape(block.shape)

    def apply_one(field):
        return coarse_apply(field, tiles_one, columns_one, live_one)

    def restrict_one(field):
        return segment_total(field, coarse_groups, C2)

    def prolong_one(coarse):
        return jnp.take(coarse, coarse_groups, axis=1)

    def apply_two(field):
        return coarse_apply(field, tiles_two, columns_two, live_two)

    def restrict_two(field):
        return segment_total(field, coarser_groups, C3L)

    def prolong_two(coarse):
        return jnp.take(coarse, coarser_groups, axis=1)

    def chain_solve(right):
        grouped = gather_directly(right, "narrow", 1)
        piece_now = grouped.T
        forward_map = chain_forward[0]
        back_map = chain_backward[0]
        start_term = jnp.dot(chain_gain[0], piece_now, precision=lax.Precision.HIGHEST)
        identity = (jnp.eye(piece_now.shape[0], dtype=jnp.float32), jnp.zeros_like(piece_now))
        before = entering((forward_map, start_term), WIDE, compose, identity, False)
        ahead_value = jnp.dot(forward_map, before[1], precision=lax.Precision.HIGHEST) + start_term
        beyond = entering((back_map, ahead_value), WIDE, compose, identity, True)
        behind_value = jnp.dot(back_map, beyond[1], precision=lax.Precision.HIGHEST) + ahead_value
        own_rows = right.shape[1]
        mine = lax.dynamic_slice_in_dim(
            behind_value, lax.axis_index("narrow") * own_rows, own_rows, 0
        )
        return mine.T

    diag_one = jnp.diagonal(tiles_one[:, 0], axis1=1, axis2=2).reshape(-1)
    diag_two = jnp.diagonal(tiles_two[:, 0], axis1=1, axis2=2).reshape(-1)
    levels = (
        (apply_fine, fine_diagonal, restrict_fine, prolong_fine),
        (apply_one, diag_one, restrict_one, prolong_one),
        (apply_two, diag_two, restrict_two, prolong_two),
    )
    return smooth_cycle(0, block, levels, chain_solve)


def solution(mesh):
    split = Mesh(
        mesh.devices.reshape(4, 8, 2, mesh.shape["narrow"]),
        ("wide_0", "wide_1", "wide_2", "narrow"),
    )
    placed = (
        P(None, WIDE, "narrow"),
        P(WIDE, "narrow"),
        P(WIDE, "narrow"),
        P(WIDE, "narrow"),
        P(WIDE_NARROW, None, None, None),
        P(WIDE_NARROW, None),
        P(WIDE_NARROW, None),
        P(WIDE_NARROW),
        P(WIDE_NARROW, None, None, None),
        P(WIDE_NARROW, None),
        P(WIDE_NARROW, None),
        P(WIDE_NARROW),
        P(WIDE, None, None),
        P(WIDE, None, None),
        P(WIDE, None, None),
    )
    return jax.shard_map(
        body, mesh=split, in_specs=placed, out_specs=P(None, WIDE, "narrow"), check_vma=False
    )
```

profile of v0, /device:TPU:2, one launch (start us, length us, event | category | flops | bytes accessed | tf_op | source)
XLA Modules:
  0.0 685.4 jit_solution(6325326655473349025)
XLA Ops:
  3.9 3.5 collective-permute-start.1
  17.6 4.6 collective-permute-start.5
  22.2 6.3 collective-permute-start.2
  30.5 5.0 collective-permute-done.3
  37.3 4.6 collective-permute-start.9
  46.3 4.6 collective-permute-done.7
  53.3 5.3 collective-permute-start.13
  62.9 4.7 copy.788
  70.8 4.7 copy.919
  75.5 87.9 %scatter_custom_fusion = f32[2048,4]{1,0:T(8,128)S(1)} fusion(s32[16384]{0:T(1024)S(1)} %bitcast.722, f32[16384,4]{1,0:T(8,128)} %bitcast.679, f32[]{:T(128)} %constant.170.clone.1), kind=kCustom, calls=%fused_computation.130 | custom fusion | flops 65536 | bytes 33280 | tf_op jit(solution)/shard_map/scatter-add | solution.py:156
  165.7 5.8 collective-permute-start.15
  172.2 3.5 all-to-all-start
  175.7 5.9 all-to-all-done
  182.4 5.3 fusion.12
  192.7 5.8 collective-permute-start.17
  199.1 3.5 all-to-all-start.1
  202.6 5.9 all-to-all-done.1
  209.3 5.3 fusion.15
  223.3 5.7 collective-permute-start.19
  229.7 3.3 all-to-all-start.2
  233.1 5.9 all-to-all-done.2
  239.8 5.4 fusion.18
  249.5 11.9 %scatter_custom_fusion.1 = f32[256,4]{1,0:T(8,128)S(1)} fusion(s32[2048]{0:T(1024)S(1)} %copy-done.7, f32[2048,4]{1,0:T(8,128)} %copy.801, f32[]{:T(128)} %constant.170.clone.1), kind=kCustom, calls=%fused_computation.465 | custom fusion | flops 8192 | bytes 4608 | tf_op jit(solution)/shard_map/scatter-add | solution.py:156
  263.6 5.8 collective-permute-start.21
  270.0 3.5 all-to-all-start.3
  273.6 5.2 all-to-all-done.3
  283.2 5.8 collective-permute-start.23
  289.7 3.3 all-to-all-start.4
  293.0 5.3 all-to-all-done.4
  302.7 5.8 collective-permute-start.25
  312.5 5.3 all-to-all-done.5
  325.7 5.0 all-to-all-done.6
  336.0 25.4 %all-gather.7 = f32[8,132,128]{2,1,0:T(8,128)S(1)} all-gather(f32[1,132,128]{2,1,0:T(8,128)S(1)} %maximum_bitcast_fusion.1), channel_id=3, replica_groups=mesh['wide_0'=4,'wide_1'=8,'wide_2'=2,'narrow'=4] {'wide_1'}, dimensions={0}, use_global_device_ids=true | all-gather | bytes 608256 | tf_op jit(solution)/shard_map/all_gather | solution.py:78
  367.3 12.6 %all-gather.8 = f32[4,132,128]{2,1,0:T(8,128)S(1)} all-gather(f32[1,132,128]{2,1,0:T(8,128)S(1)} %maximum_bitcast_fusion.2), channel_id=4, replica_groups=mesh['wide_0'=4,'wide_1'=8,'wide_2'=2,'narrow'=4] {'wide_0'}, dimensions={0}, use_global_device_ids=true | all-gather | bytes 337920 | tf_op jit(solution)/shard_map/all_gather | solution.py:78
  385.9 25.9 %all-gather.10 = f32[8,132,128]{2,1,0:T(8,128)S(1)} all-gather(f32[1,132,128]{2,1,0:T(8,128)S(1)} %maximum_bitcast_fusion.4), channel_id=6, replica_groups=mesh['wide_0'=4,'wide_1'=8,'wide_2'=2,'narrow'=4] {'wide_1'}, dimensions={0}, use_global_device_ids=true | all-gather | bytes 608256 | tf_op jit(solution)/shard_map/all_gather | solution.py:78
  417.7 12.3 %all-gather.11 = f32[4,132,128]{2,1,0:T(8,128)S(1)} all-gather(f32[1,132,128]{2,1,0:T(8,128)S(1)} %maximum_bitcast_fusion.5), channel_id=7, replica_groups=mesh['wide_0'=4,'wide_1'=8,'wide_2'=2,'narrow'=4] {'wide_0'}, dimensions={0}, use_global_device_ids=true | all-gather | bytes 337920 | tf_op jit(solution)/shard_map/all_gather | solution.py:78
  435.3 5.8 collective-permute-start.27
  441.8 3.3 all-to-all-start.7
  445.2 5.2 all-to-all-done.7
  454.7 5.8 collective-permute-start.29
  464.5 5.3 all-to-all-done.8
  474.2 5.8 collective-permute-start.31
  484.0 5.3 all-to-all-done.9
  491.7 5.5 gather_fusion.3
  499.5 5.8 collective-permute-start.33
  505.9 3.5 all-to-all-start.10
  509.5 5.9 all-to-all-done.10
  516.2 5.3 fusion.21
  526.4 5.8 collective-permute-start.35
  532.9 3.3 all-to-all-start.11
  536.2 5.9 all-to-all-done.11
  542.9 5.3 fusion.24
  553.2 5.8 collective-permute-start.37
  559.6 3.5 all-to-all-start.12
  563.2 5.9 all-to-all-done.12
  569.9 5.3 fusion.27
  578.6 54.8 %gather_fusion.4 = f32[16384,4]{1,0:T(8,128)} fusion(f32[4,2048]{0,1:T(8,128)S(1)} %copy.900, s32[16384]{0:T(1024)S(1)} %broadcast_clamp_fusion), kind=kCustom, calls=%fused_computation.16 | custom fusion | bytes 589824 | tf_op jit(solution)/shard_map/jit(_take)/gather | solution.py:225
  633.3 5.2 copy.901
  640.1 4.6 collective-permute-start.41
  649.0 4.6 collective-permute-done.39
  655.3 4.6 collective-permute-start.45
  664.3 4.6 collective-permute-done.43
  670.6 4.6 collective-permute-start.49
  679.6 4.6 collective-permute-done.47
  (468 shorter events, 167.1 us)
Async XLA Ops:
  0.0 332.1 %copy-start = (f32[1,128,128]{2,1,0:T(8,128)S(1)}, f32[1,128,128]{2,1,0:T(8,128)}, u32[]{:S(2)}) copy-start(f32[1,128,128]{2,1,0:T(8,128)} %param.32) | copy-start | bytes 196612
  1.0 13.2 %collective-permute-start = (f32[1,128]{1,0:T(1,128)S(1)}, f32[1,128]{1,0:T(1,128)S(1)}, u32[]{:S(2)}, u32[]{:S(2)}) collective-permute-start(f32[1,128]{1,0:T(1,128)S(1)} %slice.624), channel_id=1, source_target_pairs={{0,4},{4,8},{8,12},{12,16},{16,20},{20,24},{24,28},{28,32},{32,36}... | collective-permute-start | bytes 1544 | tf_op jit(solution)/shard_map/ppermute | solution.py:41
  3.9 10.3 %collective-permute-start.1 = (f32[128,1]{1,0:T(8,128)S(1)}, f32[128,1]{1,0:T(8,128)S(1)}, u32[]{:S(2)}, u32[]{:S(2)}) collective-permute-start(f32[128,1]{1,0:T(8,128)S(1)} %slice.626), channel_id=1, source_target_pairs={{0,1},{1,2},{2,3},{4,5},{5,6},{6,7},{8,9},{9,10},{10,11},{12,13},{... | collective-permute-start | bytes 1544 | tf_op jit(solution)/shard_map/ppermute | solution.py:41
  16.3 14.2 %collective-permute-start.4 = (f32[4,128,1]{2,1,0:T(8,128)S(1)}, f32[4,128,1]{2,1,0:T(8,128)S(1)}, u32[]{:S(2)}, u32[]{:S(2)}) collective-permute-start(f32[4,128,1]{2,1,0:T(8,128)S(1)} %get-tuple-element.56), channel_id=1, source_target_pairs={{1,0},{2,1},{3,2},{5,4},{6,5},{7,6},{9,8},{10,9},{11,10},{13,12},{... | collective-permute-start | bytes 6152 | tf_op jit(solution)/shard_map/ppermute | solution.py:53
  17.6 12.9 %collective-permute-start.5 = (f32[4,128,1]{2,1,0:T(8,128)S(1)}, f32[4,128,1]{2,1,0:T(8,128)S(1)}, u32[]{:S(2)}, u32[]{:S(2)}) collective-permute-start(f32[4,128,1]{2,1,0:T(8,128)S(1)} %get-tuple-element.57), channel_id=1, source_target_pairs={{0,1},{1,2},{2,3},{4,5},{5,6},{6,7},{8,9},{9,10},{10,11},{12,13},{... | collective-permute-start | bytes 6152 | tf_op jit(solution)/shard_map/ppermute | solution.py:52
  22.2 8.3 %collective-permute-start.2 = (f32[4,1,128]{2,1,0:T(1,128)S(1)}, f32[4,1,128]{2,1,0:T(1,128)S(1)}, u32[]{:S(2)}, u32[]{:S(2)}) collective-permute-start(f32[4,1,128]{2,1,0:T(1,128)S(1)} %get-tuple-element.59), channel_id=1, source_target_pairs={{4,0},{8,4},{12,8},{16,12},{20,16},{24,20},{28,24},{32,28},{36,32}... | collective-permute-start | bytes 6152 | tf_op jit(solution)/shard_map/ppermute | solution.py:53
  28.6 7.0 %collective-permute-start.3 = (f32[4,1,128]{2,1,0:T(1,128)S(1)}, f32[4,1,128]{2,1,0:T(1,128)S(1)}, u32[]{:S(2)}, u32[]{:S(2)}) collective-permute-start(f32[4,1,128]{2,1,0:T(1,128)S(1)} %get-tuple-element.58), channel_id=1, source_target_pairs={{0,4},{4,8},{8,12},{12,16},{16,20},{20,24},{24,28},{28,32},{32,36}... | collective-permute-start | bytes 6152 | tf_op jit(solution)/shard_map/ppermute | solution.py:52
  36.0 10.2 %collective-permute-start.8 = (f32[4,128,1]{2,1,0:T(8,128)S(1)}, f32[4,128,1]{2,1,0:T(8,128)S(1)}, u32[]{:S(2)}, u32[]{:S(2)}) collective-permute-start(f32[4,128,1]{2,1,0:T(8,128)S(1)} %get-tuple-element.52), channel_id=1, source_target_pairs={{1,0},{2,1},{3,2},{5,4},{6,5},{7,6},{9,8},{10,9},{11,10},{13,12},{... | collective-permute-start | bytes 6152 | tf_op jit(solution)/shard_map/ppermute | solution.py:53
  37.3 8.9 %collective-permute-start.9 = (f32[4,128,1]{2,1,0:T(8,128)S(1)}, f32[4,128,1]{2,1,0:T(8,128)S(1)}, u32[]{:S(2)}, u32[]{:S(2)}) collective-permute-start(f32[4,128,1]{2,1,0:T(8,128)S(1)} %get-tuple-element.53), channel_id=1, source_target_pairs={{0,1},{1,2},{2,3},{4,5},{5,6},{6,7},{8,9},{9,10},{10,11},{12,13},{... | collective-permute-start | bytes 6152 | tf_op jit(solution)/shard_map/ppermute | solution.py:52
  41.9 4.4 collective-permute-start.6
  43.8 7.0 %collective-permute-start.7 = (f32[4,1,128]{2,1,0:T(1,128)S(1)}, f32[4,1,128]{2,1,0:T(1,128)S(1)}, u32[]{:S(2)}, u32[]{:S(2)}) collective-permute-start(f32[4,1,128]{2,1,0:T(1,128)S(1)} %get-tuple-element.54), channel_id=1, source_target_pairs={{0,4},{4,8},{8,12},{12,16},{16,20},{20,24},{24,28},{28,32},{32,36}... | collective-permute-start | bytes 6152 | tf_op jit(solution)/shard_map/ppermute | solution.py:52
  52.0 17.5 %collective-permute-start.12 = (f32[4,128,1]{2,1,0:T(8,128)}, f32[4,128,1]{2,1,0:T(8,128)S(1)}, u32[]{:S(2)}, u32[]{:S(2)}) collective-permute-start(f32[4,128,1]{2,1,0:T(8,128)} %get-tuple-element.48), channel_id=1, source_target_pairs={{1,0},{2,1},{3,2},{5,4},{6,5},{7,6},{9,8},{10,9},{11,10},{13,12},{... | collective-permute-start | bytes 6152 | tf_op jit(solution)/shard_map/ppermute | solution.py:53
  53.3 16.2 %collective-permute-start.13 = (f32[4,128,1]{2,1,0:T(8,128)}, f32[4,128,1]{2,1,0:T(8,128)}, u32[]{:S(2)}, u32[]{:S(2)}) collective-permute-start(f32[4,128,1]{2,1,0:T(8,128)} %get-tuple-element.49), channel_id=1, source_target_pairs={{0,1},{1,2},{2,3},{4,5},{5,6},{6,7},{8,9},{9,10},{10,11},{12,13},{... | collective-permute-start | bytes 6152 | tf_op jit(solution)/shard_map/ppermute | solution.py:52
  58.6 11.0 %collective-permute-start.10 = (f32[4,1,128]{2,1,0:T(1,128)S(1)}, f32[4,1,128]{2,1,0:T(1,128)S(1)}, u32[]{:S(2)}, u32[]{:S(2)}) collective-permute-start(f32[4,1,128]{2,1,0:T(1,128)S(1)} %get-tuple-element.51), channel_id=1, source_target_pairs={{4,0},{8,4},{12,8},{16,12},{20,16},{24,20},{28,24},{32,28},{36,32}... | collective-permute-start | bytes 6152 | tf_op jit(solution)/shard_map/ppermute | solution.py:53
  60.5 9.0 %collective-permute-start.11 = (f32[4,1,128]{2,1,0:T(1,128)S(1)}, f32[4,1,128]{2,1,0:T(1,128)S(1)}, u32[]{:S(2)}, u32[]{:S(2)}) collective-permute-start(f32[4,1,128]{2,1,0:T(1,128)S(1)} %get-tuple-element.50), channel_id=1, source_target_pairs={{0,4},{4,8},{8,12},{12,16},{16,20},{20,24},{24,28},{28,32},{32,36}... | collective-permute-start | bytes 6152 | tf_op jit(solution)/shard_map/ppermute | solution.py:52
  163.8 11.9 %collective-permute-start.14 = (f32[4,2048]{1,0:T(4,128)S(1)}, f32[4,2048]{1,0:T(4,128)S(1)}, u32[]{:S(2)}, u32[]{:S(2)}) collective-permute-start(f32[4,2048]{1,0:T(4,128)S(1)} %fusion.272), channel_id=1, source_target_pairs={{0,4},{4,8},{8,12},{12,16},{16,20},{20,24},{24,28},{28,32},{32,36}... | collective-permute-start | bytes 98312 | tf_op jit(solution)/shard_map/ppermute | solution.py:41
  165.7 9.9 %collective-permute-start.15 = (f32[4,2048]{1,0:T(4,128)S(1)}, f32[4,2048]{1,0:T(4,128)S(1)}, u32[]{:S(2)}, u32[]{:S(2)}) collective-permute-start(f32[4,2048]{1,0:T(4,128)S(1)} %fusion.272), channel_id=1, source_target_pairs={{4,0},{8,4},{12,8},{16,12},{20,16},{24,20},{28,24},{32,28},{36,32}... | collective-permute-start | bytes 98312 | tf_op jit(solution)/shard_map/ppermute | solution.py:41
  172.2 9.5 %all-to-all-start = ((f32[4,1,4,2048]{3,2,1,0:T(4,128)}), f32[4,1,4,2048]{3,2,1,0:T(4,128)S(1)}, u32[]{:S(2)}, u32[]{:S(2)}) async-start(f32[4,1,4,2048]{3,2,1,0:T(4,128)} %broadcast_in_dim.126), calls=%async_computation | async-start | bytes 262144 | tf_op jit(solution)/shard_map/all_to_all | solution.py:22
  190.7 11.9 %collective-permute-start.16 = (f32[4,2048]{1,0:T(4,128)S(1)}, f32[4,2048]{1,0:T(4,128)S(1)}, u32[]{:S(2)}, u32[]{:S(2)}) collective-permute-start(f32[4,2048]{1,0:T(4,128)S(1)} %get-tuple-element.77), channel_id=1, source_target_pairs={{0,4},{4,8},{8,12},{12,16},{16,20},{20,24},{24,28},{28,32},{32,36}... | collective-permute-start | bytes 98312 | tf_op jit(solution)/shard_map/ppermute | solution.py:41
  192.7 10.0 %collective-permute-start.17 = (f32[4,2048]{1,0:T(4,128)S(1)}, f32[4,2048]{1,0:T(4,128)S(1)}, u32[]{:S(2)}, u32[]{:S(2)}) collective-permute-start(f32[4,2048]{1,0:T(4,128)S(1)} %get-tuple-element.77), channel_id=1, source_target_pairs={{4,0},{8,4},{12,8},{16,12},{20,16},{24,20},{28,24},{32,28},{36,32}... | collective-permute-start | bytes 98312 | tf_op jit(solution)/shard_map/ppermute | solution.py:41
  199.1 9.4 %all-to-all-start.1 = ((f32[4,1,4,2048]{3,2,1,0:T(4,128)}), f32[4,1,4,2048]{3,2,1,0:T(4,128)S(1)}, u32[]{:S(2)}, u32[]{:S(2)}) async-start(f32[4,1,4,2048]{3,2,1,0:T(4,128)} %broadcast_in_dim.218), calls=%async_computation.1 | async-start | bytes 262144 | tf_op jit(solution)/shard_map/all_to_all | solution.py:22
  217.7 15.4 %collective-permute-start.18 = (f32[4,2048]{1,0:T(4,128)S(1)}, f32[4,2048]{1,0:T(4,128)S(1)}, u32[]{:S(2)}, u32[]{:S(2)}) collective-permute-start(f32[4,2048]{1,0:T(4,128)S(1)} %broadcast_divide_fusion.2), channel_id=1, source_target_pairs={{0,4},{4,8},{8,12},{12,16},{16,20},{20,24},{24,28},{28,32},{32,36}... | collective-permute-start | bytes 98312 | tf_op jit(solution)/shard_map/ppermute | solution.py:41
  223.3 9.8 %collective-permute-start.19 = (f32[4,2048]{1,0:T(4,128)S(1)}, f32[4,2048]{1,0:T(4,128)S(1)}, u32[]{:S(2)}, u32[]{:S(2)}) collective-permute-start(f32[4,2048]{1,0:T(4,128)S(1)} %broadcast_divide_fusion.2), channel_id=1, source_target_pairs={{4,0},{8,4},{12,8},{16,12},{20,16},{24,20},{28,24},{32,28},{36,32}... | collective-permute-start | bytes 98312 | tf_op jit(solution)/shard_map/ppermute | solution.py:41
  229.7 9.3 %all-to-all-start.2 = ((f32[4,1,4,2048]{3,2,1,0:T(4,128)}), f32[4,1,4,2048]{3,2,1,0:T(4,128)S(1)}, u32[]{:S(2)}, u32[]{:S(2)}) async-start(f32[4,1,4,2048]{3,2,1,0:T(4,128)} %broadcast_in_dim.219), calls=%async_computation.2 | async-start | bytes 262144 | tf_op jit(solution)/shard_map/all_to_all | solution.py:22
  261.5 12.0 %collective-permute-start.20 = (f32[4,256]{0,1:T(8,128)S(1)}, f32[4,256]{0,1:T(8,128)S(1)}, u32[]{:S(2)}, u32[]{:S(2)}) collective-permute-start(f32[4,256]{0,1:T(8,128)S(1)} %fusion.195), channel_id=1, source_target_pairs={{0,4},{4,8},{8,12},{12,16},{16,20},{20,24},{24,28},{28,32},{32,36}... | collective-permute-start | bytes 12296 | tf_op jit(solution)/shard_map/ppermute | solution.py:41
  263.6 10.0 %collective-permute-start.21 = (f32[4,256]{0,1:T(8,128)S(1)}, f32[4,256]{0,1:T(8,128)S(1)}, u32[]{:S(2)}, u32[]{:S(2)}) collective-permute-start(f32[4,256]{0,1:T(8,128)S(1)} %fusion.195), channel_id=1, source_target_pairs={{4,0},{8,4},{12,8},{16,12},{20,16},{24,20},{28,24},{32,28},{36,32}... | collective-permute-start | bytes 12296 | tf_op jit(solution)/shard_map/ppermute | solution.py:41
  270.0 8.8 %all-to-all-start.3 = ((f32[4,1,4,256]{3,2,1,0:T(4,128)}), f32[4,1,4,256]{3,2,1,0:T(4,128)S(1)}, u32[]{:S(2)}, u32[]{:S(2)}) async-start(f32[4,1,4,256]{3,2,1,0:T(4,128)} %broadcast_in_dim.220), calls=%async_computation.3 | async-start | bytes 32768 | tf_op jit(solution)/shard_map/all_to_all | solution.py:22
  281.3 11.7 %collective-permute-start.22 = (f32[4,256]{0,1:T(8,128)S(1)}, f32[4,256]{0,1:T(8,128)S(1)}, u32[]{:S(2)}, u32[]{:S(2)}) collective-permute-start(f32[4,256]{0,1:T(8,128)S(1)} %get-tuple-element.81), channel_id=1, source_target_pairs={{0,4},{4,8},{8,12},{12,16},{16,20},{20,24},{24,28},{28,32},{32,36}... | collective-permute-start | bytes 12296 | tf_op jit(solution)/shard_map/ppermute | solution.py:41
  283.2 9.8 %collective-permute-start.23 = (f32[4,256]{0,1:T(8,128)S(1)}, f32[4,256]{0,1:T(8,128)S(1)}, u32[]{:S(2)}, u32[]{:S(2)}) collective-permute-start(f32[4,256]{0,1:T(8,128)S(1)} %get-tuple-element.81), channel_id=1, source_target_pairs={{4,0},{8,4},{12,8},{16,12},{20,16},{24,20},{28,24},{32,28},{36,32}... | collective-permute-start | bytes 12296 | tf_op jit(solution)/shard_map/ppermute | solution.py:41
  289.7 8.6 %all-to-all-start.4 = ((f32[4,1,4,256]{3,2,1,0:T(4,128)}), f32[4,1,4,256]{3,2,1,0:T(4,128)S(1)}, u32[]{:S(2)}, u32[]{:S(2)}) async-start(f32[4,1,4,256]{3,2,1,0:T(4,128)} %broadcast_in_dim.224), calls=%async_computation.4 | async-start | bytes 32768 | tf_op jit(solution)/shard_map/all_to_all | solution.py:22
  300.8 11.7 %collective-permute-start.24 = (f32[4,256]{0,1:T(8,128)S(1)}, f32[4,256]{0,1:T(8,128)S(1)}, u32[]{:S(2)}, u32[]{:S(2)}) collective-permute-start(f32[4,256]{0,1:T(8,128)S(1)} %get-tuple-element.83), channel_id=1, source_target_pairs={{0,4},{4,8},{8,12},{12,16},{16,20},{20,24},{24,28},{28,32},{32,36}... | collective-permute-start | bytes 12296 | tf_op jit(solution)/shard_map/ppermute | solution.py:41
  302.7 9.8 %collective-permute-start.25 = (f32[4,256]{0,1:T(8,128)S(1)}, f32[4,256]{0,1:T(8,128)S(1)}, u32[]{:S(2)}, u32[]{:S(2)}) collective-permute-start(f32[4,256]{0,1:T(8,128)S(1)} %get-tuple-element.83), channel_id=1, source_target_pairs={{4,0},{8,4},{12,8},{16,12},{20,16},{24,20},{28,24},{32,28},{36,32}... | collective-permute-start | bytes 12296 | tf_op jit(solution)/shard_map/ppermute | solution.py:41
  309.2 8.6 %all-to-all-start.5 = ((f32[4,1,4,256]{3,2,1,0:T(4,128)}), f32[4,1,4,256]{3,2,1,0:T(4,128)S(1)}, u32[]{:S(2)}, u32[]{:S(2)}) async-start(f32[4,1,4,256]{3,2,1,0:T(4,128)} %broadcast_in_dim.225), calls=%async_computation.5 | async-start | bytes 32768 | tf_op jit(solution)/shard_map/all_to_all | solution.py:22
  322.4 8.4 %all-to-all-start.6 = ((f32[4,1,128]{2,1,0:T(1,128)}), f32[4,1,128]{2,1,0:T(1,128)S(1)}, u32[]{:S(2)}, u32[]{:S(2)}) async-start(f32[4,1,128]{2,1,0:T(1,128)} %reshape.822), calls=%async_computation.6 | async-start | bytes 4096 | tf_op jit(solution)/shard_map/all_to_all | solution.py:22
  433.3 11.9 %collective-permute-start.26 = (f32[4,256]{0,1:T(8,128)S(1)}, f32[4,256]{0,1:T(8,128)S(1)}, u32[]{:S(2)}, u32[]{:S(2)}) collective-permute-start(f32[4,256]{0,1:T(8,128)S(1)} %bitcast_select_fusion.1), channel_id=1, source_target_pairs={{0,4},{4,8},{8,12},{12,16},{16,20},{20,24},{24,28},{28,32},{32,36}... | collective-permute-start | bytes 12296 | tf_op jit(solution)/shard_map/ppermute | solution.py:41
  435.3 9.8 %collective-permute-start.27 = (f32[4,256]{0,1:T(8,128)S(1)}, f32[4,256]{0,1:T(8,128)S(1)}, u32[]{:S(2)}, u32[]{:S(2)}) collective-permute-start(f32[4,256]{0,1:T(8,128)S(1)} %bitcast_select_fusion.1), channel_id=1, source_target_pairs={{4,0},{8,4},{12,8},{16,12},{20,16},{24,20},{28,24},{32,28},{36,32}... | collective-permute-start | bytes 12296 | tf_op jit(solution)/shard_map/ppermute | solution.py:41
  441.8 8.6 %all-to-all-start.7 = ((f32[4,1,4,256]{3,2,1,0:T(4,128)}), f32[4,1,4,256]{3,2,1,0:T(4,128)S(1)}, u32[]{:S(2)}, u32[]{:S(2)}) async-start(f32[4,1,4,256]{3,2,1,0:T(4,128)} %broadcast_in_dim.235), calls=%async_computation.7 | async-start | bytes 32768 | tf_op jit(solution)/shard_map/all_to_all | solution.py:22
  452.8 11.7 %collective-permute-start.28 = (f32[4,256]{0,1:T(8,128)S(1)}, f32[4,256]{0,1:T(8,128)S(1)}, u32[]{:S(2)}, u32[]{:S(2)}) collective-permute-start(f32[4,256]{0,1:T(8,128)S(1)} %get-tuple-element.85), channel_id=1, source_target_pairs={{0,4},{4,8},{8,12},{12,16},{16,20},{20,24},{24,28},{28,32},{32,36}... | collective-permute-start | bytes 12296 | tf_op jit(solution)/shard_map/ppermute | solution.py:41
  454.7 9.8 %collective-permute-start.29 = (f32[4,256]{0,1:T(8,128)S(1)}, f32[4,256]{0,1:T(8,128)S(1)}, u32[]{:S(2)}, u32[]{:S(2)}) collective-permute-start(f32[4,256]{0,1:T(8,128)S(1)} %get-tuple-element.85), channel_id=1, source_target_pairs={{4,0},{8,4},{12,8},{16,12},{20,16},{24,20},{28,24},{32,28},{36,32}... | collective-permute-start | bytes 12296 | tf_op jit(solution)/shard_map/ppermute | solution.py:41
  461.2 8.6 %all-to-all-start.8 = ((f32[4,1,4,256]{3,2,1,0:T(4,128)}), f32[4,1,4,256]{3,2,1,0:T(4,128)S(1)}, u32[]{:S(2)}, u32[]{:S(2)}) async-start(f32[4,1,4,256]{3,2,1,0:T(4,128)} %broadcast_in_dim.236), calls=%async_computation.8 | async-start | bytes 32768 | tf_op jit(solution)/shard_map/all_to_all | solution.py:22
  472.3 11.7 %collective-permute-start.30 = (f32[4,256]{0,1:T(8,128)S(1)}, f32[4,256]{0,1:T(8,128)S(1)}, u32[]{:S(2)}, u32[]{:S(2)}) collective-permute-start(f32[4,256]{0,1:T(8,128)S(1)} %get-tuple-element.87), channel_id=1, source_target_pairs={{0,4},{4,8},{8,12},{12,16},{16,20},{20,24},{24,28},{28,32},{32,36}... | collective-permute-start | bytes 12296 | tf_op jit(solution)/shard_map/ppermute | solution.py:41
  474.2 9.8 %collective-permute-start.31 = (f32[4,256]{0,1:T(8,128)S(1)}, f32[4,256]{0,1:T(8,128)S(1)}, u32[]{:S(2)}, u32[]{:S(2)}) collective-permute-start(f32[4,256]{0,1:T(8,128)S(1)} %get-tuple-element.87), channel_id=1, source_target_pairs={{4,0},{8,4},{12,8},{16,12},{20,16},{24,20},{28,24},{32,28},{36,32}... | collective-permute-start | bytes 12296 | tf_op jit(solution)/shard_map/ppermute | solution.py:41
  480.7 8.6 %all-to-all-start.9 = ((f32[4,1,4,256]{3,2,1,0:T(4,128)}), f32[4,1,4,256]{3,2,1,0:T(4,128)S(1)}, u32[]{:S(2)}, u32[]{:S(2)}) async-start(f32[4,1,4,256]{3,2,1,0:T(4,128)} %broadcast_in_dim.237), calls=%async_computation.9 | async-start | bytes 32768 | tf_op jit(solution)/shard_map/all_to_all | solution.py:22
  497.6 11.9 %collective-permute-start.32 = (f32[4,2048]{1,0:T(4,128)S(1)}, f32[4,2048]{1,0:T(4,128)S(1)}, u32[]{:S(2)}, u32[]{:S(2)}) collective-permute-start(f32[4,2048]{1,0:T(4,128)S(1)} %bitcast_select_fusion.5), channel_id=1, source_target_pairs={{0,4},{4,8},{8,12},{12,16},{16,20},{20,24},{24,28},{28,32},{32,36}... | collective-permute-start | bytes 98312 | tf_op jit(solution)/shard_map/ppermute | solution.py:41
  499.5 10.0 %collective-permute-start.33 = (f32[4,2048]{1,0:T(4,128)S(1)}, f32[4,2048]{1,0:T(4,128)S(1)}, u32[]{:S(2)}, u32[]{:S(2)}) collective-permute-start(f32[4,2048]{1,0:T(4,128)S(1)} %bitcast_select_fusion.5), channel_id=1, source_target_pairs={{4,0},{8,4},{12,8},{16,12},{20,16},{24,20},{28,24},{32,28},{36,32}... | collective-permute-start | bytes 98312 | tf_op jit(solution)/shard_map/ppermute | solution.py:41
  505.9 9.4 %all-to-all-start.10 = ((f32[4,1,4,2048]{3,2,1,0:T(4,128)}), f32[4,1,4,2048]{3,2,1,0:T(4,128)S(1)}, u32[]{:S(2)}, u32[]{:S(2)}) async-start(f32[4,1,4,2048]{3,2,1,0:T(4,128)} %broadcast_in_dim.245), calls=%async_computation.10 | async-start | bytes 262144 | tf_op jit(solution)/shard_map/all_to_all | solution.py:22
  524.5 11.7 %collective-permute-start.34 = (f32[4,2048]{1,0:T(4,128)S(1)}, f32[4,2048]{1,0:T(4,128)S(1)}, u32[]{:S(2)}, u32[]{:S(2)}) collective-permute-start(f32[4,2048]{1,0:T(4,128)S(1)} %get-tuple-element.89), channel_id=1, source_target_pairs={{0,4},{4,8},{8,12},{12,16},{16,20},{20,24},{24,28},{28,32},{32,36}... | collective-permute-start | bytes 98312 | tf_op jit(solution)/shard_map/ppermute | solution.py:41
  526.4 9.8 %collective-permute-start.35 = (f32[4,2048]{1,0:T(4,128)S(1)}, f32[4,2048]{1,0:T(4,128)S(1)}, u32[]{:S(2)}, u32[]{:S(2)}) collective-permute-start(f32[4,2048]{1,0:T(4,128)S(1)} %get-tuple-element.89), channel_id=1, source_target_pairs={{4,0},{8,4},{12,8},{16,12},{20,16},{24,20},{28,24},{32,28},{36,32}... | collective-permute-start | bytes 98312 | tf_op jit(solution)/shard_map/ppermute | solution.py:41
  532.9 9.3 %all-to-all-start.11 = ((f32[4,1,4,2048]{3,2,1,0:T(4,128)}), f32[4,1,4,2048]{3,2,1,0:T(4,128)S(1)}, u32[]{:S(2)}, u32[]{:S(2)}) async-start(f32[4,1,4,2048]{3,2,1,0:T(4,128)} %broadcast_in_dim.246), calls=%async_computation.11 | async-start | bytes 262144 | tf_op jit(solution)/shard_map/all_to_all | solution.py:22
  551.2 11.9 %collective-permute-start.36 = (f32[4,2048]{1,0:T(4,128)S(1)}, f32[4,2048]{1,0:T(4,128)S(1)}, u32[]{:S(2)}, u32[]{:S(2)}) collective-permute-start(f32[4,2048]{1,0:T(4,128)S(1)} %get-tuple-element.91), channel_id=1, source_target_pairs={{0,4},{4,8},{8,12},{12,16},{16,20},{20,24},{24,28},{28,32},{32,36}... | collective-permute-start | bytes 98312 | tf_op jit(solution)/shard_map/ppermute | solution.py:41
  553.2 10.0 %collective-permute-start.37 = (f32[4,2048]{1,0:T(4,128)S(1)}, f32[4,2048]{1,0:T(4,128)S(1)}, u32[]{:S(2)}, u32[]{:S(2)}) collective-permute-start(f32[4,2048]{1,0:T(4,128)S(1)} %get-tuple-element.91), channel_id=1, source_target_pairs={{4,0},{8,4},{12,8},{16,12},{20,16},{24,20},{28,24},{32,28},{36,32}... | collective-permute-start | bytes 98312 | tf_op jit(solution)/shard_map/ppermute | solution.py:41
  559.6 9.5 %all-to-all-start.12 = ((f32[4,1,4,2048]{3,2,1,0:T(4,128)}), f32[4,1,4,2048]{3,2,1,0:T(4,128)S(1)}, u32[]{:S(2)}, u32[]{:S(2)}) async-start(f32[4,1,4,2048]{3,2,1,0:T(4,128)} %broadcast_in_dim.247), calls=%async_computation.12 | async-start | bytes 262144 | tf_op jit(solution)/shard_map/all_to_all | solution.py:22
  638.8 10.2 %collective-permute-start.40 = (f32[4,128,1]{2,1,0:T(8,128)S(1)}, f32[4,128,1]{2,1,0:T(8,128)S(1)}, u32[]{:S(2)}, u32[]{:S(2)}) collective-permute-start(f32[4,128,1]{2,1,0:T(8,128)S(1)} %get-tuple-element.44), channel_id=1, source_target_pairs={{1,0},{2,1},{3,2},{5,4},{6,5},{7,6},{9,8},{10,9},{11,10},{13,12},{... | collective-permute-start | bytes 6152 | tf_op jit(solution)/shard_map/ppermute | solution.py:53
  640.1 8.9 %collective-permute-start.41 = (f32[4,128,1]{2,1,0:T(8,128)S(1)}, f32[4,128,1]{2,1,0:T(8,128)S(1)}, u32[]{:S(2)}, u32[]{:S(2)}) collective-permute-start(f32[4,128,1]{2,1,0:T(8,128)S(1)} %get-tuple-element.45), channel_id=1, source_target_pairs={{0,1},{1,2},{2,3},{4,5},{5,6},{6,7},{8,9},{9,10},{10,11},{12,13},{... | collective-permute-start | bytes 6152 | tf_op jit(solution)/shard_map/ppermute | solution.py:52
  644.6 4.4 collective-permute-start.38
  646.6 7.0 %collective-permute-start.39 = (f32[4,1,128]{2,1,0:T(1,128)S(1)}, f32[4,1,128]{2,1,0:T(1,128)S(1)}, u32[]{:S(2)}, u32[]{:S(2)}) collective-permute-start(f32[4,1,128]{2,1,0:T(1,128)S(1)} %get-tuple-element.46), channel_id=1, source_target_pairs={{0,4},{4,8},{8,12},{12,16},{16,20},{20,24},{24,28},{28,32},{32,36}... | collective-permute-start | bytes 6152 | tf_op jit(solution)/shard_map/ppermute | solution.py:52
  654.0 10.2 %collective-permute-start.44 = (f32[4,128,1]{2,1,0:T(8,128)S(1)}, f32[4,128,1]{2,1,0:T(8,128)S(1)}, u32[]{:S(2)}, u32[]{:S(2)}) collective-permute-start(f32[4,128,1]{2,1,0:T(8,128)S(1)} %get-tuple-element.40), channel_id=1, source_target_pairs={{1,0},{2,1},{3,2},{5,4},{6,5},{7,6},{9,8},{10,9},{11,10},{13,12},{... | collective-permute-start | bytes 6152 | tf_op jit(solution)/shard_map/ppermute | solution.py:53
  655.3 8.9 %collective-permute-start.45 = (f32[4,128,1]{2,1,0:T(8,128)S(1)}, f32[4,128,1]{2,1,0:T(8,128)S(1)}, u32[]{:S(2)}, u32[]{:S(2)}) collective-permute-start(f32[4,128,1]{2,1,0:T(8,128)S(1)} %get-tuple-element.41), channel_id=1, source_target_pairs={{0,1},{1,2},{2,3},{4,5},{5,6},{6,7},{8,9},{9,10},{10,11},{12,13},{... | collective-permute-start | bytes 6152 | tf_op jit(solution)/shard_map/ppermute | solution.py:52
  659.9 4.4 collective-permute-start.42
  661.8 7.0 %collective-permute-start.43 = (f32[4,1,128]{2,1,0:T(1,128)S(1)}, f32[4,1,128]{2,1,0:T(1,128)S(1)}, u32[]{:S(2)}, u32[]{:S(2)}) collective-permute-start(f32[4,1,128]{2,1,0:T(1,128)S(1)} %get-tuple-element.42), channel_id=1, source_target_pairs={{0,4},{4,8},{8,12},{12,16},{16,20},{20,24},{24,28},{28,32},{32,36}... | collective-permute-start | bytes 6152 | tf_op jit(solution)/shard_map/ppermute | solution.py:52
  669.3 10.2 %collective-permute-start.48 = (f32[4,128,1]{2,1,0:T(8,128)S(1)}, f32[4,128,1]{2,1,0:T(8,128)S(1)}, u32[]{:S(2)}, u32[]{:S(2)}) collective-permute-start(f32[4,128,1]{2,1,0:T(8,128)S(1)} %get-tuple-element.36), channel_id=1, source_target_pairs={{1,0},{2,1},{3,2},{5,4},{6,5},{7,6},{9,8},{10,9},{11,10},{13,12},{... | collective-permute-start | bytes 6152 | tf_op jit(solution)/shard_map/ppermute | solution.py:53
  670.6 8.9 %collective-permute-start.49 = (f32[4,128,1]{2,1,0:T(8,128)S(1)}, f32[4,128,1]{2,1,0:T(8,128)S(1)}, u32[]{:S(2)}, u32[]{:S(2)}) collective-permute-start(f32[4,128,1]{2,1,0:T(8,128)S(1)} %get-tuple-element.37), channel_id=1, source_target_pairs={{0,1},{1,2},{2,3},{4,5},{5,6},{6,7},{8,9},{9,10},{10,11},{12,13},{... | collective-permute-start | bytes 6152 | tf_op jit(solution)/shard_map/ppermute | solution.py:52
  675.2 4.4 collective-permute-start.46
  677.1 7.0 %collective-permute-start.47 = (f32[4,1,128]{2,1,0:T(1,128)S(1)}, f32[4,1,128]{2,1,0:T(1,128)S(1)}, u32[]{:S(2)}, u32[]{:S(2)}) collective-permute-start(f32[4,1,128]{2,1,0:T(1,128)S(1)} %get-tuple-element.38), channel_id=1, source_target_pairs={{0,4},{4,8},{8,12},{12,16},{16,20},{20,24},{24,28},{28,32},{32,36}... | collective-permute-start | bytes 6152 | tf_op jit(solution)/shard_map/ppermute | solution.py:52
  (8 other events, 323.9 us)
where the time goes:
time: 696 us; the launch traced here: 685 us
  starting transfers between devices  207 us (30%)
  local copies, waits for them, and re-layouts  118 us (17%)
  other arithmetic  115 us (17%)
  waiting for transfers between devices  95.3 us (14%)
  blocking collectives  80 us (11%)
  matrix products  68 us (10%)
    scatter-add x3, other arithmetic, segment_total(): return jax.ops.segment_sum(values.T, indices, num_segments=segment_count).T  101 us
    ppermute x26, starting transfers between devices, shifted(): return lax.ppermute(block, axis, route)  97.5 us
    all_gather x6, blocking collectives, gathered_once(): both, at, found = (lax.all_gather(jnp.concatenate(lines), axis), 0, {})  80 us
    all_to_all x13, waiting for transfers between devices, sent_to_all(): lax.all_to_all(jnp.broadcast_to(shard[None], (peers, *shard.shape)), axis...  71.9 us
    gather x2, local copies, waits for them, and re-layouts, prolong_fine(): return jnp.take(coarse, fine_ids, axis=1).reshape(block.shape)  60 us
    all_to_all x13, starting transfers between devices, sent_to_all(): lax.all_to_all(jnp.broadcast_to(shard[None], (peers, *shard.shape)), axis...  43.6 us
    ppermute x12, starting transfers between devices, with_halo(): lax.ppermute(last, axis, up)  42 us
    dot_general x12, matrix products, tile_product(): jnp.einsum('rkab,crkb->cra', tiles[:, 1:], picked, precision=lax.Precisio...  35.4 us
  transfers between devices with their start and end apart: 63, of which 18 were waited for; matrix products, arithmetic and copies ran while one was open for 4% of the time, Pallas kernels for 0%

commit v1 on v0

v1 whole, which is shorter than its diff:
```python
import jax
import jax.numpy as jnp
from jax import lax
from jax.experimental import pallas as pl
from jax.experimental.pallas import tpu as pltpu
from jax.sharding import PartitionSpec as P

F32 = jnp.float32
BF16 = jnp.bfloat16
MESH_ID = pl.DeviceIdType.MESH
GX = 128
GY = 128
COLS = 4
NT1 = 16
NT2 = 4
C3L = 32
CORES = 2
CHIPS_Z = 8
TOP = 16
EXT_ROWS = 160
EXT_LANES = 256
WEST, EAST, SOUTH, NORTH = 0, 1, 2, 3
STEPS = ((-1, 0), (1, 0), (0, -1), (0, 1), (-1, -1), (-1, 1), (1, -1), (1, 1))
FACING = (1, 0, 3, 2, 7, 6, 5, 4)
shift_value = 0.1
jacobi_weight = 0.6
smooth_weight = 0.5


def iota(shape, dim):
    return lax.broadcasted_iota(jnp.int32, shape, dim)


def dot_nt(a, b):
    return lax.dot_general(a, b, (((1,), (1,)), ((), ())), preferred_element_type=F32)


def dot_nn(a, b):
    return lax.dot_general(a, b, (((1,), (0,)), ((), ())), preferred_element_type=F32)


def matmul(a, b):
    return jnp.dot(a, b, precision=lax.Precision.HIGHEST, preferred_element_type=F32)


def upper():
    return iota((8, 128), 0) < 4


def left():
    return iota((8, 128), 1) < 64


def rounded(v):
    return v.astype(BF16).astype(F32)


def fold(o):
    return o + pltpu.roll(o, 4, 0)


def split_twin(v):
    hi = rounded(v)
    return jnp.where(upper(), hi, v - hi)


def split_pair(v):
    hi = rounded(v)
    lo = v - hi
    first = jnp.where(upper(), hi, pltpu.roll(lo, 4, 0))
    second = jnp.where(upper(), pltpu.roll(hi, 4, 0), lo)
    return first, second


def store_split(ref, m):
    hi = m.astype(BF16)
    ref[:, 0:128] = hi
    ref[:, 128:256] = (m - hi.astype(F32)).astype(BF16)


def times(v, split_map):
    a = split_twin(v).astype(BF16)
    return fold(dot_nt(jnp.concatenate([a, a], axis=1), split_map))


def kernel(
    wide_size,
    narrow_size,
    block,
    east,
    north,
    fine_groups,
    tiles_one,
    columns_one,
    live_one,
    coarse_groups,
    tiles_two,
    columns_two,
    live_two,
    coarser_groups,
    chain_forward,
    chain_gain,
    chain_backward,
    out,
    ext,
    groups_hi,
    groups_lo,
    held_one,
    held_two,
    slabs,
    packs,
    fine_box,
    weight_e,
    weight_w,
    weight_n,
    weight_s,
    inverse,
    diagonal,
    field_a,
    field_b,
    field_c,
    second,
    high_rows,
    low_rows,
    segment,
    table,
    w_one,
    w_two,
    picks_one,
    picks_two,
    spots_one,
    spots_two,
    hot_one,
    hot_two,
    sent_one,
    sent_two,
    box_one,
    box_two,
    pair_maps,
    pair_split,
    own_split,
    z_maps,
    z_split,
    prefix_u,
    suffix_v,
    x_maps,
    x_split,
    last_split,
    box_rhs,
    box_z,
    box_x,
    enter_y,
    enter_x,
    local_sem,
    fine_send,
    fine_recv,
    send_one,
    recv_one,
    send_two,
    recv_two,
    core_send,
    core_recv,
    rhs_send,
    rhs_recv,
    zmap_send,
    zmap_recv,
    xmap_send,
    xmap_recv,
    z_send,
    z_recv,
    x_send,
    x_recv,
):
    w = lax.axis_index("wide")
    q = lax.axis_index("narrow")
    seg_size = CORES * CHIPS_Z
    segs = wide_size // seg_size
    xs = w // seg_size
    zs = lax.rem(w, seg_size) // CORES
    core = lax.rem(w, CORES)

    def place(step):
        return w + step[0], q + step[1]

    def exists(step):
        a, b = place(step)
        return (a >= 0) & (a < wide_size) & (b >= 0) & (b < narrow_size)

    loads = (
        (block, ext.at[pl.ds(0, 4), pl.ds(TOP, GX), pl.ds(0, GY)]),
        (east, ext.at[4, pl.ds(TOP, GX), pl.ds(0, GY)]),
        (north, ext.at[5, pl.ds(TOP, GX), pl.ds(0, GY)]),
        (chain_forward.at[0], pair_maps.at[core, 0]),
        (chain_gain.at[0], pair_maps.at[core, 1]),
        (chain_backward.at[0], pair_maps.at[core, 2]),
        (fine_groups, groups_lo),
        (tiles_two, held_two),
        (tiles_one, held_one),
    )
    local = [pltpu.make_async_copy(a, b, local_sem.at[i]) for i, (a, b) in enumerate(loads)]
    for c in local:
        c.start()

    barrier = pltpu.get_barrier_semaphore()
    awaited = jnp.int32(0)
    for step in STEPS:
        there = exists(step)
        a, b = place(step)

        @pl.when(there)
        def _():
            pl.semaphore_signal(barrier, inc=1, device_id=(a, b), device_id_type=MESH_ID)

        awaited = awaited + jnp.where(there, 1, 0)
    group = [(i, j) for i in range(CORES) for j in range(narrow_size)]
    for i, j in group[1:]:
        mate = (w - core + lax.rem(core + i, CORES), lax.rem(q + j, narrow_size))
        pl.semaphore_signal(barrier, inc=1, device_id=mate, device_id_type=MESH_ID)
    for i in range(1, CHIPS_Z):
        mate = (xs * seg_size + lax.rem(zs + i, CHIPS_Z) * CORES + core, q)
        pl.semaphore_signal(barrier, inc=1, device_id=mate, device_id_type=MESH_ID)
    for i in range(1, segs):
        mate = (lax.rem(xs + i, segs) * seg_size + zs * CORES + core, q)
        pl.semaphore_signal(barrier, inc=1, device_id=mate, device_id_type=MESH_ID)
    awaited = awaited + len(group) - 1 + CHIPS_Z - 1 + segs - 1

    def fine_start(turn, source, arrays):
        lane = iota((8, 128), 1) // 4
        for a in range(arrays):
            slabs[turn, 0, a] = source[a, TOP : TOP + 8, 0:128]
            slabs[turn, 1, a] = source[a, TOP + GX - 8 : TOP + GX, 0:128]
            packed = jnp.zeros((8, 128), F32)
            for g in range(GX // 8):
                v = source[a, TOP + 8 * g : TOP + 8 * g + 8, 0:128]
                packed = jnp.where(lane == g, v if g == 0 else pltpu.roll(v, 4 * g, 1), packed)
                packed = jnp.where(lane == 16 + g, pltpu.roll(v, (68 + 4 * g) % 128, 1), packed)
            packs[turn, a] = packed

    def fine_copy(turn, arrays, d, landing):
        span = pl.ds(0, arrays)
        source = slabs.at[turn, d, span] if d < 2 else packs.at[turn, span]
        return pltpu.make_async_remote_copy(
            src_ref=source,
            dst_ref=fine_box.at[turn, landing, span],
            send_sem=fine_send.at[turn, d],
            recv_sem=fine_recv.at[turn, landing],
            device_id=place(STEPS[d]),
            device_id_type=MESH_ID,
        )

    def fine_send_all(turn, arrays):
        for d, step in enumerate(STEPS):

            @pl.when(exists(step))
            def _():
                fine_copy(turn, arrays, d, FACING[d]).start()

    def fine_wait(turn, arrays):
        for d, step in enumerate(STEPS):

            @pl.when(exists(step))
            def _():
                fine_copy(turn, arrays, d, d).wait_recv()
                fine_copy(turn, arrays, d, FACING[d]).wait_send()

    def fine_fill(turn, target, arrays):
        lane = iota((8, 128), 1)
        there = [exists(step) for step in STEPS]

        def got(d, a):
            return jnp.where(there[d], fine_box[turn, d, a], 0.0)

        def beside(south_pack, south_group, north_pack, north_group):
            low = pltpu.roll(south_pack, (124 - 64 - 4 * south_group) % 128, 1)
            high = pltpu.roll(north_pack, (128 - 4 * north_group) % 128, 1)
            return jnp.where(lane < 4, high, jnp.where(lane >= 124, low, 0.0))

        for a in range(arrays):
            target[a, TOP - 8 : TOP, 0:128] = got(0, a)
            target[a, TOP + GX : TOP + GX + 8, 0:128] = got(1, a)
            south_pack, north_pack = got(2, a), got(3, a)
            for g in range(GX // 8):
                target[a, TOP + 8 * g : TOP + 8 * g + 8, 128:256] = beside(south_pack, g, north_pack, g)
            target[a, TOP - 8 : TOP, 128:256] = beside(got(4, a), 15, got(5, a), 15)
            target[a, TOP + GX : TOP + GX + 8, 128:256] = beside(got(6, a), 0, got(7, a), 0)

    local[0].wait()
    local[1].wait()
    local[2].wait()
    fine_start(0, ext, 6)
    pl.semaphore_wait(barrier, awaited)
    fine_send_all(0, 6)

    local[3].wait()
    local[4].wait()
    local[5].wait()

    def core_copy(landing):
        return pltpu.make_async_remote_copy(
            src_ref=pair_maps.at[core],
            dst_ref=pair_maps.at[landing],
            send_sem=core_send,
            recv_sem=core_recv,
            device_id=(w - core + (1 - core), q),
            device_id_type=MESH_ID,
        )

    core_copy(core).start()

    local[6].wait()
    groups = groups_lo[...]
    groups_hi[...] = groups // 128
    groups_lo[...] = lax.rem(groups, 128)
    for r in range(NT1):
        for k in range(3):
            spots_one[3 * r + k] = jnp.where(live_one[r, k] == 1, columns_one[r, k], 5 * NT1)
    for r in range(NT2):
        for k in range(3):
            spots_two[3 * r + k] = jnp.where(live_two[r, k] == 1, columns_two[r, k], 5 * NT2)
    picks_one[5 * NT1] = jnp.zeros((8, 128), F32)
    picks_two[5 * NT2] = jnp.zeros((8, 128), F32)
    local[7].wait()
    lane_two = iota((64, 128), 1)
    eye_two = iota((64, 128), 0) == lax.rem(lane_two, 64)
    diag_two = []
    for r in range(NT2):
        for k in range(4):
            m = held_two[r, k]
            m = jnp.concatenate([m, m], axis=1)
            if k == 0:
                diag_two.append(jnp.sum(jnp.where(eye_two, m, 0.0), axis=0, keepdims=True))
            hi = rounded(m)
            m = jnp.where(lane_two < 64, hi, m - hi).astype(BF16)
            w_two[r, 0:64, 128 * k : 128 * k + 128] = m
            w_two[r, 64:128, 128 * k : 128 * k + 128] = m
    wide_two = [jnp.broadcast_to(d, (8, 128)) for d in diag_two]
    inverse_two = 1.0 / jnp.where(
        upper(),
        jnp.where(left(), wide_two[0], wide_two[1]),
        jnp.where(left(), wide_two[2], wide_two[3]),
    )
    for t in range(NT1):
        hot = iota((256, 128), 0) == coarse_groups[t : t + 1, :]
        hot_one[:, 128 * t : 128 * t + 128] = jnp.where(hot, 1.0, 0.0).astype(BF16)
    for h in range(2):
        hot = iota((128, 128), 0) == coarser_groups[h : h + 1, :] + C3L * q
        hot_two[:, 128 * h : 128 * h + 128] = jnp.where(hot, 1.0, 0.0).astype(BF16)
    local[8].wait()

    eye_one = iota((128, 128), 0) == iota((128, 128), 1)

    def split_tiles(t, carry):
        diags = []
        for r in (t, t + 8):
            for k in range(4):
                m = held_one[r, k]
                if k == 0:
                    diags.append(jnp.sum(jnp.where(eye_one, m, 0.0), axis=0, keepdims=True))
                store_split(w_one.at[r, :, pl.ds(256 * k, 256)], m)
        low, high = (jnp.broadcast_to(d, (8, 128)) for d in diags)
        table[t] = 1.0 / jnp.where(upper(), low, high)
        return carry

    lax.fori_loop(0, 8, split_tiles, 0)
    inverse_one = table[...]

    fine_wait(0, 6)
    fine_fill(0, ext, 6)
    rows_all = range(8, EXT_ROWS - 8, 8)
    last_row = wide_size * GX - 1
    last_column = narrow_size * GY - 1
    lane_ext = iota((8, EXT_LANES), 1)
    column = q * GY + jnp.where(lane_ext < 192, lane_ext, lane_ext - EXT_LANES)
    for o in rows_all:
        row = w * GX + (o - TOP) + iota((8, EXT_LANES), 0)
        ext[4, o : o + 8, :] = jnp.where(row < last_row, ext[4, o : o + 8, :], 0.0)
        ext[5, o : o + 8, :] = jnp.where(column < last_column, ext[5, o : o + 8, :], 0.0)
    for o in rows_all:
        e = ext[4, o : o + 8, :]
        b = ext[4, o - 1 : o + 7, :]
        n = ext[5, o : o + 8, :]
        s = pltpu.roll(n, 1, 1)
        d = shift_value + e + b + n + s
        inv = 1.0 / d
        weight_e[o - 8 : o, :] = e * inv
        weight_w[o - 8 : o, :] = b * inv
        weight_n[o - 8 : o, :] = n * inv
        weight_s[o - 8 : o, :] = s * inv
        if TOP <= o < TOP + GX:
            diagonal[o - TOP : o - TOP + 8, :] = d[:, 0:128]
        for c in range(COLS):
            field_a[c, o : o + 8, :] = ext[c, o : o + 8, :] * inv

    def mixed(source, c, o):
        v = source[c, o : o + 8, :]
        a = weight_e[o - 8 : o, :] * source[c, o + 1 : o + 9, :]
        b = weight_w[o - 8 : o, :] * source[c, o - 1 : o + 7, :]
        n = weight_n[o - 8 : o, :] * pltpu.roll(v, EXT_LANES - 1, 1)
        s = weight_s[o - 8 : o, :] * pltpu.roll(v, 1, 1)
        return v, (a + b) + (n + s)

    rows_in = range(TOP, TOP + GX, 8)
    rest = 1.0 - jacobi_weight
    for o in rows_all:
        for c in range(COLS):
            v, m = mixed(field_a, c, o)
            field_b[c, o : o + 8, :] = rest * v + jacobi_weight * m
    for o in rows_all:
        for c in range(COLS):
            v, m = mixed(field_b, c, o)
            field_c[c, o : o + 8, :] = rest * v + jacobi_weight * m
    for o in rows_in:
        i = o - TOP
        for c in range(COLS):
            v, m = mixed(field_c, c, o)
            r = ((1.0 - smooth_weight) * v + smooth_weight * m)[:, 0:128] * diagonal[i : i + 8, :]
            both = field_a[c, o : o + 8, 0:128] + field_b[c, o : o + 8, 0:128]
            second[c, i : i + 8, :] = jacobi_weight * both
            hi = rounded(r)
            lo = r - hi
            for h in range(2):
                high_rows[pl.ds(8 * i + 4 * h + c, 8, stride=8), :] = hi
                low_rows[pl.ds(8 * i + 4 * h + c, 8, stride=8), :] = lo

    segment[...] = jnp.zeros((128, 128), F32)
    half = jnp.where(upper(), 0, 8)
    tall = iota((128, 128), 0)
    chunk = 8

    def gather_up(step, carry):
        lhs, rhs = [], []
        for j in range(chunk):
            i = step * chunk + j
            hi_index = jnp.broadcast_to(groups_hi[pl.ds(i, 1), :], (8, 128))
            lo_index = groups_lo[pl.ds(i, 1), :]
            at = pl.multiple_of(8 * i, 8)
            v_hi = high_rows[pl.ds(at, 8), :]
            v_lo = low_rows[pl.ds(at, 8), :]
            masks = [hi_index == half + t for t in range(8)]
            rows = [jnp.where(m, v_hi, 0.0) for m in masks] + [jnp.where(m, v_lo, 0.0) for m in masks]
            lhs.append(jnp.concatenate(rows, axis=0).astype(BF16))
            rhs.append(jnp.where(tall == lo_index, 1.0, 0.0).astype(BF16))
        segment[...] += dot_nt(jnp.concatenate(lhs, axis=1), jnp.concatenate(rhs, axis=1))
        return carry

    lax.fori_loop(0, GX // chunk, gather_up, 0)
    right_one = (segment[0:64, :] + segment[64:128, :]).reshape(8, 8, 128)

    def coarse_copy(sent, box, sends, receives, k, d, landing):
        return pltpu.make_async_remote_copy(
            src_ref=sent.at[k],
            dst_ref=box.at[k, landing],
            send_sem=sends.at[k, d],
            recv_sem=receives.at[k, landing],
            device_id=place(STEPS[d]),
            device_id_type=MESH_ID,
        )

    def coarse_send(bufs, k):
        for d in range(4):

            @pl.when(exists(STEPS[d]))
            def _():
                coarse_copy(*bufs, k, d, FACING[d]).start()

    def coarse_wait(bufs, k):
        for d in range(4):

            @pl.when(exists(STEPS[d]))
            def _():
                coarse_copy(*bufs, k, d, d).wait_recv()
                coarse_copy(*bufs, k, d, FACING[d]).wait_send()

    bufs_one = (sent_one, box_one, send_one, recv_one)
    bufs_two = (sent_two, box_two, send_two, recv_two)

    def put_one(p, t, v):
        a, b = split_pair(v)
        picks_one[NT1 * p + t] = a
        picks_one[NT1 * p + t + 8] = b

    def apply_one(k, field, meanwhile=None):
        sent_one[k] = field
        coarse_send(bufs_one, k)
        for t in range(8):
            put_one(0, t, field[t])
        own = []
        for r in range(NT1):
            a = picks_one[r].astype(BF16)
            own.append(dot_nt(jnp.concatenate([a, a], axis=1), w_one[r, :, 0:256]))
        own = [jnp.where(upper(), fold(own[t]), fold(own[t + 8])) for t in range(8)]
        if meanwhile is not None:
            meanwhile()
        coarse_wait(bufs_one, k)
        for d in range(4):
            there = exists(STEPS[d])
            for t in range(8):
                put_one(d + 1, t, jnp.where(there, box_one[k, d, t], 0.0))
        outs = []
        for r in range(NT1):
            parts = []
            for j in range(3):
                a = picks_one[spots_one[3 * r + j]].astype(BF16)
                parts += [a, a]
            outs.append(dot_nt(jnp.concatenate(parts, axis=1), w_one[r, :, 256:1024]))
        return jnp.stack(
            [own[t] + jnp.where(upper(), fold(outs[t]), fold(outs[t + 8])) for t in range(8)]
        )

    def put_two(p, v):
        for h, a in enumerate(split_pair(v)):
            turned = pltpu.roll(a, 64, 1)
            picks_two[NT2 * p + 2 * h] = jnp.where(left(), a, turned)
            picks_two[NT2 * p + 2 * h + 1] = jnp.where(left(), turned, a)

    def apply_two(k, field, meanwhile=None):
        sent_two[k] = field
        coarse_send(bufs_two, k)
        put_two(0, field)
        if meanwhile is not None:
            meanwhile()
        coarse_wait(bufs_two, k)
        for d in range(4):
            put_two(d + 1, jnp.where(exists(STEPS[d]), box_two[k, d], 0.0))
        outs = []
        for r in range(NT2):
            parts = [picks_two[r]] + [picks_two[spots_two[3 * r + j]] for j in range(3)]
            lhs = jnp.concatenate([a.astype(BF16) for a in parts], axis=1)
            outs.append(fold(dot_nt(lhs, w_two[r])))
        return jnp.where(
            upper(), jnp.where(left(), outs[0], outs[1]), jnp.where(left(), outs[2], outs[3])
        )

    def down(apply_op, inv, right, windows):
        s0 = inv * right
        r1 = right - jacobi_weight * apply_op(0, s0, windows[0])
        s1 = inv * r1
        r2 = r1 - jacobi_weight * apply_op(1, s1, windows[1])
        s2 = inv * r2
        r3 = r2 - smooth_weight * apply_op(2, s2, windows[2])
        return r3, r2, jacobi_weight * (s0 + s1)

    def up(apply_op, inv, spread, r2, x2):
        fix = spread - smooth_weight * (inv * apply_op(3, spread))
        r3 = r2 - apply_op(4, fix)
        s3 = inv * r3
        r4 = r3 - jacobi_weight * apply_op(5, s3)
        return x2 + fix + jacobi_weight * s3 + jacobi_weight * (inv * r4)

    def peer_copy(source, target, sends, receives, slot, landing, mate):
        return pltpu.make_async_remote_copy(
            src_ref=source,
            dst_ref=target.at[landing],
            send_sem=sends.at[slot],
            recv_sem=receives.at[landing],
            device_id=mate,
            device_id_type=MESH_ID,
        )

    def z_mate(i):
        z = lax.rem(zs + i, CHIPS_Z)
        return z, (xs * seg_size + z * CORES + core, q)

    def x_mate(i):
        x = lax.rem(xs + i, segs)
        return x, (x * seg_size + zs * CORES + core, q)

    def along(mates, count, box, sends, receives, mine):
        def start():
            for i in range(1, count):
                _, mate = mates(i)
                peer_copy(box.at[mine], box, sends, receives, i, mine, mate).start()

        def finish():
            for i in range(1, count):
                other, mate = mates(i)
                peer_copy(box.at[mine], box, sends, receives, i, other, mate).wait_recv()
                peer_copy(box.at[mine], box, sends, receives, i, mine, mate).wait_send()

        return start, finish

    zmap_start, zmap_finish = along(z_mate, CHIPS_Z, z_maps, zmap_send, zmap_recv, zs)
    xmap_start, xmap_finish = along(x_mate, segs, x_maps, xmap_send, xmap_recv, xs)
    z_start, z_finish = along(z_mate, CHIPS_Z, box_z, z_send, z_recv, zs)
    x_start, x_finish = along(x_mate, segs, box_x, x_send, x_recv, xs)

    def pair_products():
        core_copy(1 - core).wait_recv()
        core_copy(core).wait_send()
        f0, g0, b0 = pair_maps[0, 0], pair_maps[0, 1], pair_maps[0, 2]
        f1, g1, b1 = pair_maps[1, 0], pair_maps[1, 1], pair_maps[1, 2]
        both = matmul(f1, f0)
        z_maps[zs, 0] = both
        z_maps[zs, 1] = f0 + matmul(b0, both)
        z_maps[zs, 2] = matmul(b0, b1)
        zmap_start()

    def pair_gains():
        g0, b0 = pair_maps[0, 1], pair_maps[0, 2]
        f1, g1 = pair_maps[1, 0], pair_maps[1, 1]
        across = matmul(f1, g0)
        store_split(pair_split.at[0:128, 0:256], across)
        store_split(pair_split.at[0:128, 256:512], g1)
        store_split(pair_split.at[128:256, 0:256], g0 + matmul(b0, across))
        store_split(pair_split.at[128:256, 256:512], matmul(b0, g1))

    def z_prefix():
        zmap_finish()
        prefix_u[0] = jnp.where(eye_one, 1.0, 0.0)
        prefix_u[1] = z_maps[0, 0]

        def one(p, carry):
            prefix_u[p + 1] = matmul(z_maps[p, 0], prefix_u[p])
            return carry

        lax.fori_loop(1, CHIPS_Z, one, 0)
        x_maps[xs, 0] = prefix_u[CHIPS_Z]

    def z_suffix():
        suffix_v[CHIPS_Z, :, 0:128] = jnp.zeros((128, 128), F32)
        suffix_v[CHIPS_Z, :, 128:256] = jnp.where(eye_one, 1.0, 0.0)

        def one(i, carry):
            p = CHIPS_Z - 1 - i
            both = matmul(z_maps[p, 2], suffix_v[p + 1])
            suffix_v[p, :, 0:128] = both[:, 0:128] + matmul(z_maps[p, 1], prefix_u[p])
            suffix_v[p, :, 128:256] = both[:, 128:256]
            return carry

        lax.fori_loop(0, CHIPS_Z, one, 0)
        x_maps[xs, 1] = suffix_v[0, :, 0:128]
        x_maps[xs, 2] = suffix_v[0, :, 128:256]
        xmap_start()

    def z_splits():
        def one(p, carry):
            for j in range(3):
                store_split(z_split.at[p, j], z_maps[p, j])
            return carry

        lax.fori_loop(0, CHIPS_Z, one, 0)
        inner = core == 0
        first = jnp.where(inner, z_maps[zs, 1], z_maps[zs, 0])
        last = jnp.where(inner, z_maps[zs, 2], pair_maps[1, 2])
        store_split(own_split.at[:, 0:256], first)
        store_split(own_split.at[:, 256:512], last)
        both = matmul(last, suffix_v[zs + 1])
        store_split(last_split.at[:, 0:256], matmul(first, prefix_u[zs]) + both[:, 0:128])
        store_split(last_split.at[:, 256:512], both[:, 128:256])

    def x_splits():
        xmap_finish()
        for p in range(segs):
            for j in range(3):
                store_split(x_split.at[p, j], x_maps[p, j])

    def joined(a, b):
        a, b = split_twin(a).astype(BF16), split_twin(b).astype(BF16)
        return jnp.concatenate([a, a, b, b], axis=1)

    def sweep(count, maps, box):
        y = box[0, 0]
        enter_y[0] = jnp.zeros((8, 128), F32)
        lifted = [box[0, 1]]
        for p in range(1, count):
            enter_y[p] = y
            lifted.append(box[p, 1] + times(y, maps[p, 1]))
            y = box[p, 0] + times(y, maps[p, 0])
        x = lifted[count - 1]
        enter_x[count - 1] = jnp.zeros((8, 128), F32)
        for p in reversed(range(count - 1)):
            enter_x[p] = x
            x = lifted[p] + times(x, maps[p, 2])
        return y, x

    def chain_solve(piece):
        slot = core * narrow_size + q
        box_rhs[slot] = piece

        def rhs_copy(i, j, landing):
            mate = (w - core + lax.rem(core + i, CORES), lax.rem(q + j, narrow_size))
            return peer_copy(
                box_rhs.at[slot], box_rhs, rhs_send, rhs_recv, i * narrow_size + j, landing, mate
            )

        for i, j in group[1:]:
            rhs_copy(i, j, slot).start()
        for i, j in group[1:]:
            other = lax.rem(core + i, CORES) * narrow_size + lax.rem(q + j, narrow_size)
            rhs_copy(i, j, other).wait_recv()
            rhs_copy(i, j, slot).wait_send()
        sums = []
        for i in range(CORES):
            total = box_rhs[i * narrow_size]
            for j in range(1, narrow_size):
                total = total + box_rhs[i * narrow_size + j]
            sums.append(total)
        both = fold(dot_nt(joined(*sums), pair_split[...]))
        ahead, behind = both[:, 0:128], both[:, 128:256]
        box_z[zs, 0] = ahead
        box_z[zs, 1] = behind
        z_start()
        z_finish()
        y, x = sweep(CHIPS_Z, z_split, box_z)
        box_x[xs, 0] = y
        box_x[xs, 1] = x
        x_start()
        base = jnp.where(core == 0, behind, ahead)
        base = base + fold(dot_nt(joined(enter_y[zs], enter_x[zs]), own_split[...]))
        x_finish()
        sweep(segs, x_split, box_x)
        return base + fold(dot_nt(joined(enter_y[xs], enter_x[xs]), last_split[...]))

    def halves(pair):
        return jnp.concatenate([a.astype(BF16) for a in pair], axis=1)

    def pack_two(o):
        o = fold(o)
        return jnp.where(upper(), o[:, 0:128], o[:, 128:256])

    def restrict_one(field):
        pairs = [split_pair(field[t]) for t in range(8)]
        tiles = [p[0] for p in pairs] + [p[1] for p in pairs]
        return pack_two(dot_nt(halves(tiles), hot_one[...]))

    def prolong_one(coarse):
        o = fold(dot_nn(halves(split_pair(coarse)), hot_one[...]))
        parts = [o[:, 128 * t : 128 * t + 128] for t in range(NT1)]
        return jnp.stack([jnp.where(upper(), parts[t], parts[t + 8]) for t in range(8)])

    r_one, r2_one, x2_one = down(apply_one, inverse_one, right_one, (pair_products, pair_gains, None))
    right_two = restrict_one(r_one)
    r_two, r2_two, x2_two = down(apply_two, inverse_two, right_two, (z_prefix, z_suffix, z_splits))
    piece = fold(dot_nt(halves(split_pair(r_two)), hot_two[...]))
    x_splits()
    answer = chain_solve(piece)
    spread_two = pack_two(dot_nn(split_twin(answer).astype(BF16), hot_two[...]))
    answer_two = up(apply_two, inverse_two, spread_two, r2_two, x2_two)
    answer_one = up(apply_one, inverse_one, prolong_one(answer_two), r2_one, x2_one)
    table[...] = answer_one

    def spread_rows(k, carry):
        at = pl.multiple_of(8 * k, 8)
        hi_index = groups_hi[pl.ds(at, 8), :]
        lo_index = groups_lo[pl.ds(at, 8), :]
        for c in range(COLS):
            total = jnp.zeros((8, 128), F32)
            for t in range(NT1):
                j = 4 * (t // 8) + c
                row = jnp.broadcast_to(table[t % 8, j : j + 1, :], (8, 128))
                value = jnp.take_along_axis(row, lo_index, axis=1, mode="promise_in_bounds")
                total = jnp.where(hi_index == t, value, total)
            field_a[c, pl.ds(pl.multiple_of(TOP + at, 8), 8), 0:128] = total
        return carry

    lax.fori_loop(0, GX // 8, spread_rows, 0)
    fine_start(1, field_a, 4)
    fine_send_all(1, 4)
    fine_wait(1, 4)
    fine_fill(1, field_a, 4)
    for o in rows_all:
        for c in range(COLS):
            v, m = mixed(field_a, c, o)
            field_b[c, o : o + 8, :] = (1.0 - smooth_weight) * v + smooth_weight * m
    for o in rows_all:
        for c in range(COLS):
            v, m = mixed(field_b, c, o)
            field_a[c, o : o + 8, :] = field_c[c, o : o + 8, :] - v + m
    for o in rows_in:
        i = o - TOP
        for c in range(COLS):
            v, m = mixed(field_a, c, o)
            x3 = second[c, i : i + 8, :] + field_b[c, o : o + 8, 0:128]
            s4 = rest * v + jacobi_weight * m
            out[c, i : i + 8, :] = x3 + jacobi_weight * (v + s4)[:, 0:128]


def solution(mesh):
    wide_size, narrow_size = mesh.shape["wide"], mesh.shape["narrow"]
    segs = wide_size // (CORES * CHIPS_Z)

    def body(
        block,
        east,
        north,
        fine_groups,
        tiles_one,
        columns_one,
        live_one,
        coarse_groups,
        tiles_two,
        columns_two,
        live_two,
        coarser_groups,
        chain_forward,
        chain_gain,
        chain_backward,
    ):
        hbm = pl.BlockSpec(memory_space=pl.ANY)
        vmem = pl.BlockSpec(memory_space=pltpu.VMEM)
        smem = pl.BlockSpec(memory_space=pltpu.SMEM)
        dma = pltpu.SemaphoreType.DMA
        big = pltpu.VMEM((COLS, EXT_ROWS, EXT_LANES), F32)
        weight = pltpu.VMEM((EXT_ROWS - 16, EXT_LANES), F32)
        square = pltpu.VMEM((GX, GY), F32)
        indices = pltpu.VMEM((GX, GY), jnp.int32)

        def kernel_fn(*refs):
            kernel(wide_size, narrow_size, *refs)

        return pl.pallas_call(
            kernel_fn,
            out_shape=jax.ShapeDtypeStruct((COLS, GX, GY), F32),
            in_specs=[hbm] * 5 + [smem] * 2 + [vmem, hbm] + [smem] * 2 + [vmem] + [hbm] * 3,
            out_specs=vmem,
            scratch_shapes=[
                pltpu.VMEM((6, EXT_ROWS, EXT_LANES), F32),
                indices,
                indices,
                pltpu.VMEM((NT1, 4, 128, 128), F32),
                pltpu.VMEM((NT2, 4, 64, 64), F32),
                pltpu.VMEM((2, 2, 6, 8, 128), F32),
                pltpu.VMEM((2, 6, 8, 128), F32),
                pltpu.VMEM((2, 8, 6, 8, 128), F32),
                weight,
                weight,
                weight,
                weight,
                weight,
                square,
                big,
                big,
                big,
                pltpu.VMEM((COLS, GX, GY), F32),
                pltpu.VMEM((8 * GX, GY), F32),
                pltpu.VMEM((8 * GX, GY), F32),
                square,
                pltpu.VMEM((8, 8, 128), F32),
                pltpu.VMEM((NT1, 128, 1024), BF16),
                pltpu.VMEM((NT2, 128, 512), BF16),
                pltpu.VMEM((5 * NT1 + 1, 8, 128), F32),
                pltpu.VMEM((5 * NT2 + 1, 8, 128), F32),
                pltpu.SMEM((3 * NT1,), jnp.int32),
                pltpu.SMEM((3 * NT2,), jnp.int32),
                pltpu.VMEM((256, 2048), BF16),
                pltpu.VMEM((128, 256), BF16),
                pltpu.VMEM((6, 8, 8, 128), F32),
                pltpu.VMEM((6, 8, 128), F32),
                pltpu.VMEM((6, 4, 8, 8, 128), F32),
                pltpu.VMEM((6, 4, 8, 128), F32),
                pltpu.VMEM((CORES, 3, 128, 128), F32),
                pltpu.VMEM((256, 512), BF16),
                pltpu.VMEM((128, 512), BF16),
                pltpu.VMEM((CHIPS_Z, 3, 128, 128), F32),
                pltpu.VMEM((CHIPS_Z, 3, 128, 256), BF16),
                pltpu.VMEM((CHIPS_Z + 1, 128, 128), F32),
                pltpu.VMEM((CHIPS_Z + 1, 128, 256), F32),
                pltpu.VMEM((segs, 3, 128, 128), F32),
                pltpu.VMEM((segs, 3, 128, 256), BF16),
                pltpu.VMEM((128, 512), BF16),
                pltpu.VMEM((CORES * narrow_size, 8, 128), F32),
                pltpu.VMEM((CHIPS_Z, 2, 8, 128), F32),
                pltpu.VMEM((segs, 2, 8, 128), F32),
                pltpu.VMEM((CHIPS_Z, 8, 128), F32),
                pltpu.VMEM((CHIPS_Z, 8, 128), F32),
                dma((9,)),
                dma((2, 8)),
                dma((2, 8)),
                dma((6, 4)),
                dma((6, 4)),
                dma((6, 4)),
                dma((6, 4)),
                dma,
                dma,
                dma((CORES * narrow_size,)),
                dma((CORES * narrow_size,)),
                dma((CHIPS_Z,)),
                dma((CHIPS_Z,)),
                dma((segs,)),
                dma((segs,)),
                dma((CHIPS_Z,)),
                dma((CHIPS_Z,)),
                dma((segs,)),
                dma((segs,)),
            ],
            compiler_params=pltpu.CompilerParams(
                collective_id=0, has_side_effects=True, vmem_limit_bytes=56 * 1024 * 1024
            ),
            name="cycle",
        )(
            block,
            east,
            north,
            fine_groups,
            tiles_one,
            columns_one,
            live_one,
            coarse_groups.reshape(16, 128),
            tiles_two,
            columns_two,
            live_two,
            coarser_groups.reshape(2, 128),
            chain_forward,
            chain_gain,
            chain_backward,
        )

    both = ("wide", "narrow")
    placed = (
        P(None, "wide", "narrow"),
        P("wide", "narrow"),
        P("wide", "narrow"),
        P("wide", "narrow"),
        P(both, None, None, None),
        P(both, None),
        P(both, None),
        P(both),
        P(both, None, None, None),
        P(both, None),
        P(both, None),
        P(both),
        P("wide", None, None),
        P("wide", None, None),
        P("wide", None, None),
    )
    return jax.shard_map(
        body, mesh=mesh, in_specs=placed, out_specs=P(None, "wide", "narrow"), check_vma=False
    )
```

time: 696 us -> 130 us (0.19); the launches traced: 685 us -> 130 us
  starting transfers between devices: 207 us -> 0 us
  Pallas kernels: 0 us -> 125 us
  other arithmetic: 115 us -> 0 us
  local copies, waits for them, and re-layouts: 118 us -> 4.37 us
  waiting for transfers between devices: 95.3 us -> 0 us
  blocking collectives: 80 us -> 0 us
  matrix products: 68 us -> 0 us
    ppermute x50 -> x0, starting transfers between devices: 163 us -> none  [the longest x26 97.5 us: shifted(): return lax.ppermute(block, axis, route)]
    pallas_call x0 -> x1, Pallas kernels: none -> 125 us  [body(): pl.pallas_call(kernel_fn, out_shape=jax.ShapeDtypeStruct((COLS, GX, GY),...]
    scatter-add x3 -> x0, other arithmetic: 101 us -> none  [segment_total(): return jax.ops.segment_sum(values.T, indices, num_segments=segment_count).T]
    all_gather x6 -> x0, blocking collectives: 80 us -> none  [gathered_once(): both, at, found = (lax.all_gather(jnp.concatenate(lines), axis), 0, {})]
    gather x22 -> x0, local copies, waits for them, and re-layouts: 77.4 us -> none  [the longest x2 60 us: prolong_fine(): return jnp.take(coarse, fine_ids, axis=1).reshape(block.shape)]
    all_to_all x13 -> x0, waiting for transfers between devices: 71.9 us -> none  [sent_to_all(): lax.all_to_all(jnp.broadcast_to(shard[None], (peers, *shard.shape)), axis...]
    dot_general x85 -> x0, matrix products: 68 us -> none  [the longest x12 35.4 us: tile_product(): jnp.einsum('rkab,crkb->cra', tiles[:, 1:], picked, precision=lax.Precisio...]
    all_to_all x13 -> x0, starting transfers between devices: 43.6 us -> none  [sent_to_all(): lax.all_to_all(jnp.broadcast_to(shard[None], (peers, *shard.shape)), axis...]
  transfers between devices with their start and end apart: 63 -> 0, of which waited for: 18 -> 0; matrix products, arithmetic and copies ran while one was open for 4% -> 0% of each run, Pallas kernels for 0% -> 0%
where the time goes in v1:
time: 130 us
  Pallas kernels  125 us (96%)
  local copies, waits for them, and re-layouts  4.37 us (3%)
    pallas_call x1, Pallas kernels, body(): pl.pallas_call(kernel_fn, out_shape=jax.ShapeDtypeStruct((COLS, GX, GY),...  125 us
    unnamed x3, local copies, waits for them, and re-layouts  4.37 us

profile of v1, /device:TPU:2, one launch (start us, length us, event | category | flops | bytes accessed | tf_op | source)
XLA Modules:
  0.0 129.5 jit_solution(15610249693677513717)
XLA Ops:
  0.0 1.4 %copy.16.refs_5_ = s32[16,3]{1,0:T(8,128)} copy(s32[16,3]{0,1:T(4,128)} %param.20) | data formatting | bytes 384 | tf_op args[5]
  1.4 1.3 %copy.17.refs_6_ = s32[16,3]{1,0:T(8,128)} copy(s32[16,3]{0,1:T(4,128)} %param.21) | data formatting | bytes 384 | tf_op args[6]
  2.7 125.1 %cycle.1 = f32[4,128,128]{2,1,0:T(8,128)} custom-call(f32[4,128,128]{2,1,0:T(8,128)} %refs_0_.1, f32[128,128]{1,0:T(8,128)} %refs_1_.1, f32[128,128]{1,0:T(8,128)} %refs_2_.1, s32[128,128]{1,0:T(8,128)} %refs_3_.1, f32[16,4,128,128]{3,2,1,0:T(8,128)} %refs_4_.1, s32[16,3]{1,0:T(8,128)} %copy.16.refs_5_, s32[16,3]{1,0:T(8,128)} %copy.17.refs_6_, ...), custom_call_target="tpu_custom_call" | custom-call | tf_op jit(solution)/shard_map/cycle/pallas_call | solution.py:811
  127.8 1.7 %copy.19 = f32[4,128,128]{2,1,0:T(8,128)} copy(f32[4,128,128]{2,1,0:T(8,128)} %cycle.1) | data formatting | bytes 524288

commit v2 on v1

--- a/solution.py
+++ b/solution.py
@@ -138,14 +138,18 @@
     box_two,
     pair_maps,
     pair_split,
-    own_split,
+    pair_out,
+    west_map,
+    west_split,
+    group_box,
     z_maps,
     z_split,
     prefix_u,
     suffix_v,
+    suffix_w,
     x_maps,
     x_split,
-    last_split,
+    enter_split,
     box_rhs,
     box_z,
     box_x,
@@ -160,6 +164,12 @@
     recv_two,
     core_send,
     core_recv,
+    west_send,
+    west_recv,
+    group_send,
+    group_recv,
+    relay_send,
+    relay_recv,
     rhs_send,
     rhs_recv,
     zmap_send,
@@ -305,7 +315,240 @@
             device_id_type=MESH_ID,
         )
 
+    def west_copy():
+        return pltpu.make_async_remote_copy(
+            src_ref=pair_maps.at[core, 2],
+            dst_ref=west_map,
+            send_sem=west_send,
+            recv_sem=west_recv,
+            device_id=(w + 1, q),
+            device_id_type=MESH_ID,
+        )
+
+    def group_copy(d, landing):
+        return pltpu.make_async_remote_copy(
+            src_ref=coarser_groups,
+            dst_ref=group_box.at[landing],
+            send_sem=group_send.at[d],
+            recv_sem=group_recv.at[landing],
+            device_id=place(STEPS[d]),
+            device_id_type=MESH_ID,
+        )
+
+    feeds_east = (core == CORES - 1) & (w < wide_size - 1)
+    fed_from_west = (core == 0) & (w > 0)
     core_copy(core).start()
+
+    @pl.when(feeds_east)
+    def _():
+        west_copy().start()
+
+    for d in range(4):
+
+        @pl.when(exists(STEPS[d]))
+        def _():
+            group_copy(d, FACING[d]).start()
+
+
+    eye_one = iota((128, 128), 0) == iota((128, 128), 1)
+
+    def peer_copy(source, target, sends, receives, slot, landing, mate):
+        return pltpu.make_async_remote_copy(
+            src_ref=source,
+            dst_ref=target.at[landing],
+            send_sem=sends.at[slot],
+            recv_sem=receives.at[landing],
+            device_id=mate,
+            device_id_type=MESH_ID,
+        )
+
+    def z_mate(i):
+        z = lax.rem(zs + i, CHIPS_Z)
+        return z, (xs * seg_size + z * CORES + core, q)
+
+    def x_mate(i):
+        x = lax.rem(xs + i, segs)
+        return x, (x * seg_size + zs * CORES + core, q)
+
+    def along(mates, count, box, sends, receives, mine):
+        def start():
+            for i in range(1, count):
+                _, mate = mates(i)
+                peer_copy(box.at[mine], box, sends, receives, i, mine, mate).start()
+
+        def finish():
+            for i in range(1, count):
+                other, mate = mates(i)
+                peer_copy(box.at[mine], box, sends, receives, i, other, mate).wait_recv()
+                peer_copy(box.at[mine], box, sends, receives, i, mine, mate).wait_send()
+
+        return start, finish
+
+    z_start, z_finish = along(z_mate, CHIPS_Z, box_z, z_send, z_recv, zs)
+    x_start, x_finish = along(x_mate, segs, box_x, x_send, x_recv, xs)
+    z_order = (1, 7, 2, 6, 3, 5, 4)
+
+    def zmap_copy(i, landing, mate):
+        half = pl.ds(pl.multiple_of(192 * core, 64), 192)
+        return pltpu.make_async_remote_copy(
+            src_ref=z_maps.at[zs, half],
+            dst_ref=z_maps.at[landing, half],
+            send_sem=zmap_send.at[i],
+            recv_sem=zmap_recv.at[landing],
+            device_id=mate,
+            device_id_type=MESH_ID,
+        )
+
+    def relay_copy(z, side):
+        half = pl.ds(pl.multiple_of(192 * side, 64), 192)
+        return pltpu.make_async_remote_copy(
+            src_ref=z_maps.at[z, half],
+            dst_ref=z_maps.at[z, half],
+            send_sem=relay_send.at[z],
+            recv_sem=relay_recv.at[z],
+            device_id=(w - core + (1 - core), q),
+            device_id_type=MESH_ID,
+        )
+
+    def pair_products():
+        core_copy(1 - core).wait_recv()
+        core_copy(core).wait_send()
+        f0, b0 = pair_maps[0, 0], pair_maps[0, 2]
+        f1, b1 = pair_maps[1, 0], pair_maps[1, 2]
+        both = matmul(f1, f0)
+        z_maps[zs, 0:128] = both
+        z_maps[zs, 128:256] = matmul(b0, b1)
+        z_maps[zs, 256:384] = f0 + matmul(b0, both)
+        for i in z_order:
+            _, mate = z_mate(i)
+            zmap_copy(i, zs, mate).start()
+
+    def pair_gains():
+        g0, b0 = pair_maps[0, 1], pair_maps[0, 2]
+        f1, g1 = pair_maps[1, 0], pair_maps[1, 1]
+        across = matmul(f1, g0)
+        store_split(pair_split.at[0:128, 0:256], across)
+        store_split(pair_split.at[0:128, 256:512], g1)
+        store_split(pair_split.at[128:256, 0:256], g0 + matmul(b0, across))
+        store_split(pair_split.at[128:256, 256:512], matmul(b0, g1))
+
+    def zmap_relay():
+        for i in z_order:
+            other, mate = z_mate(i)
+            zmap_copy(i, other, mate).wait_recv()
+            relay_copy(other, core).start()
+
+    def times_map(split_map, m):
+        hi = m.astype(BF16)
+        lo = (m - hi.astype(F32)).astype(BF16)
+        lhs = jnp.concatenate([split_map, split_map[:, 0:128]], axis=1)
+        return dot_nn(lhs, jnp.concatenate([hi, hi, lo], axis=0))
+
+    def z_prefix():
+        for i in z_order:
+            other, mate = z_mate(i)
+            zmap_copy(i, zs, mate).wait_send()
+            relay_copy(other, 1 - core).wait_recv()
+            relay_copy(other, core).wait_send()
+
+        def split_one(p, carry):
+            for j in range(3):
+                store_split(z_split.at[p, j], z_maps[p, 128 * j : 128 * j + 128])
+            return carry
+
+        lax.fori_loop(0, CHIPS_Z, split_one, 0)
+        one_map = jnp.where(eye_one, 1.0, 0.0)
+        prefix_u[0] = one_map
+        suffix_w[CHIPS_Z] = one_map
+
+        def one(p, carry):
+            prefix_u[p + 1] = times_map(z_split[p, 0], prefix_u[p])
+            r = CHIPS_Z - 1 - p
+            suffix_w[r] = times_map(z_split[r, 1], suffix_w[r + 1])
+            return carry
+
+        lax.fori_loop(0, CHIPS_Z, one, 0)
+        x_maps[xs, 0] = prefix_u[CHIPS_Z]
+        x_maps[xs, 1] = suffix_w[0]
+
+    def xmap_copy(part, i, landing, mate):
+        span = pl.ds(0, 2) if part == 0 else pl.ds(2, 1)
+        return pltpu.make_async_remote_copy(
+            src_ref=x_maps.at[xs, span],
+            dst_ref=x_maps.at[landing, span],
+            send_sem=xmap_send.at[part, i],
+            recv_sem=xmap_recv.at[part, landing],
+            device_id=mate,
+            device_id_type=MESH_ID,
+        )
+
+    def has_map(part, x):
+        return (x > 0) & (x < segs - 1) if part == 0 else x > 0
+
+    def z_suffix():
+        suffix_v[CHIPS_Z] = jnp.zeros((128, 128), F32)
+
+        def one(i, carry):
+            p = CHIPS_Z - 1 - i
+            suffix_v[p] = times_map(z_split[p, 1], suffix_v[p + 1]) + times_map(
+                z_split[p, 2], prefix_u[p]
+            )
+            return carry
+
+        lax.fori_loop(0, CHIPS_Z, one, 0)
+        x_maps[xs, 2] = suffix_v[0]
+        for part in range(2):
+            for i in range(1, segs):
+                _, mate = x_mate(i)
+
+                @pl.when(has_map(part, xs))
+                def _():
+                    xmap_copy(part, i, xs, mate).start()
+
+    def z_splits():
+        store_split(enter_split.at[0], prefix_u[zs])
+        store_split(enter_split.at[1], suffix_v[zs + 1])
+        store_split(enter_split.at[2], suffix_w[zs + 1])
+        pair_out[0:128, 0:256] = z_split[zs, 2]
+        pair_out[0:128, 256:512] = z_split[zs, 1]
+        pair_out[128:256, 0:256] = z_split[zs, 0]
+        store_split(pair_out.at[128:256, 256:512], pair_maps[1, 2])
+
+        @pl.when(fed_from_west)
+        def _():
+            west_copy().wait_recv()
+
+        @pl.when(feeds_east)
+        def _():
+            west_copy().wait_send()
+
+        store_split(west_split, west_map[...])
+        for d in range(4):
+
+            @pl.when(exists(STEPS[d]))
+            def _():
+                group_copy(d, d).wait_recv()
+                group_copy(d, FACING[d]).wait_send()
+
+            mark_two(d + 1, group_box[d], q + STEPS[d][1])
+
+    def x_splits():
+        for part in range(2):
+            for i in range(1, segs):
+                other, mate = x_mate(i)
+
+                @pl.when(has_map(part, other))
+                def _():
+                    xmap_copy(part, i, other, mate).wait_recv()
+
+                @pl.when(has_map(part, xs))
+                def _():
+                    xmap_copy(part, i, xs, mate).wait_send()
+
+        for p in range(1, segs):
+            for j in range(3):
+                if j == 2 or p < segs - 1:
+                    store_split(x_split.at[p, j], x_maps[p, j])
 
     local[6].wait()
     groups = groups_lo[...]
@@ -313,7 +556,7 @@
     groups_lo[...] = lax.rem(groups, 128)
     for r in range(NT1):
         for k in range(3):
-            spots_one[3 * r + k] = jnp.where(live_one[r, k] == 1, columns_one[r, k], 5 * NT1)
+            spots_one[3 * r + k] = jnp.where(live_one[k, r] == 1, columns_one[k, r], 5 * NT1)
     for r in range(NT2):
         for k in range(3):
             spots_two[3 * r + k] = jnp.where(live_two[r, k] == 1, columns_two[r, k], 5 * NT2)
@@ -342,12 +585,15 @@
     for t in range(NT1):
         hot = iota((256, 128), 0) == coarse_groups[t : t + 1, :]
         hot_one[:, 128 * t : 128 * t + 128] = jnp.where(hot, 1.0, 0.0).astype(BF16)
-    for h in range(2):
-        hot = iota((128, 128), 0) == coarser_groups[h : h + 1, :] + C3L * q
-        hot_two[:, 128 * h : 128 * h + 128] = jnp.where(hot, 1.0, 0.0).astype(BF16)
+
+    def mark_two(p, groups, owner):
+        for h in range(2):
+            hot = iota((128, 128), 0) == groups[h : h + 1, :] + C3L * owner
+            hot_two[p, :, 128 * h : 128 * h + 128] = jnp.where(hot, 1.0, 0.0).astype(BF16)
+
+    mark_two(0, coarser_groups[...], q)
+    pair_products()
     local[8].wait()
-
-    eye_one = iota((128, 128), 0) == iota((128, 128), 1)
 
     def split_tiles(t, carry):
         diags = []
@@ -363,6 +609,7 @@
 
     lax.fori_loop(0, 8, split_tiles, 0)
     inverse_one = table[...]
+    pair_gains()
 
     fine_wait(0, 6)
     fine_fill(0, ext, 6)
@@ -463,8 +710,8 @@
             def _():
                 coarse_copy(*bufs, k, d, FACING[d]).start()
 
-    def coarse_wait(bufs, k):
-        for d in range(4):
+    def coarse_wait(bufs, k, sides=range(4)):
+        for d in sides:
 
             @pl.when(exists(STEPS[d]))
             def _():
@@ -491,8 +738,8 @@
         own = [jnp.where(upper(), fold(own[t]), fold(own[t + 8])) for t in range(8)]
         if meanwhile is not None:
             meanwhile()
-        coarse_wait(bufs_one, k)
-        for d in range(4):
+        for d in (SOUTH, NORTH, WEST, EAST):
+            coarse_wait(bufs_one, k, (d,))
             there = exists(STEPS[d])
             for t in range(8):
                 put_one(d + 1, t, jnp.where(there, box_one[k, d, t], 0.0))
@@ -522,6 +769,9 @@
         coarse_wait(bufs_two, k)
         for d in range(4):
             put_two(d + 1, jnp.where(exists(STEPS[d]), box_two[k, d], 0.0))
+        return product_two()
+
+    def product_two():
         outs = []
         for r in range(NT2):
             parts = [picks_two[r]] + [picks_two[spots_two[3 * r + j]] for j in range(3)]
@@ -540,137 +790,32 @@
         r3 = r2 - smooth_weight * apply_op(2, s2, windows[2])
         return r3, r2, jacobi_weight * (s0 + s1)
 
-    def up(apply_op, inv, spread, r2, x2):
-        fix = spread - smooth_weight * (inv * apply_op(3, spread))
+    def up(apply_op, inv, spread, applied, r2, x2):
+        fix = spread - smooth_weight * (inv * applied)
         r3 = r2 - apply_op(4, fix)
         s3 = inv * r3
         r4 = r3 - jacobi_weight * apply_op(5, s3)
         return x2 + fix + jacobi_weight * s3 + jacobi_weight * (inv * r4)
 
-    def peer_copy(source, target, sends, receives, slot, landing, mate):
-        return pltpu.make_async_remote_copy(
-            src_ref=source,
-            dst_ref=target.at[landing],
-            send_sem=sends.at[slot],
-            recv_sem=receives.at[landing],
-            device_id=mate,
-            device_id_type=MESH_ID,
-        )
-
-    def z_mate(i):
-        z = lax.rem(zs + i, CHIPS_Z)
-        return z, (xs * seg_size + z * CORES + core, q)
-
-    def x_mate(i):
-        x = lax.rem(xs + i, segs)
-        return x, (x * seg_size + zs * CORES + core, q)
-
-    def along(mates, count, box, sends, receives, mine):
-        def start():
-            for i in range(1, count):
-                _, mate = mates(i)
-                peer_copy(box.at[mine], box, sends, receives, i, mine, mate).start()
-
-        def finish():
-            for i in range(1, count):
-                other, mate = mates(i)
-                peer_copy(box.at[mine], box, sends, receives, i, other, mate).wait_recv()
-                peer_copy(box.at[mine], box, sends, receives, i, mine, mate).wait_send()
-
-        return start, finish
-
-    zmap_start, zmap_finish = along(z_mate, CHIPS_Z, z_maps, zmap_send, zmap_recv, zs)
-    xmap_start, xmap_finish = along(x_mate, segs, x_maps, xmap_send, xmap_recv, xs)
-    z_start, z_finish = along(z_mate, CHIPS_Z, box_z, z_send, z_recv, zs)
-    x_start, x_finish = along(x_mate, segs, box_x, x_send, x_recv, xs)
-
-    def pair_products():
-        core_copy(1 - core).wait_recv()
-        core_copy(core).wait_send()
-        f0, g0, b0 = pair_maps[0, 0], pair_maps[0, 1], pair_maps[0, 2]
-        f1, g1, b1 = pair_maps[1, 0], pair_maps[1, 1], pair_maps[1, 2]
-        both = matmul(f1, f0)
-        z_maps[zs, 0] = both
-        z_maps[zs, 1] = f0 + matmul(b0, both)
-        z_maps[zs, 2] = matmul(b0, b1)
-        zmap_start()
-
-    def pair_gains():
-        g0, b0 = pair_maps[0, 1], pair_maps[0, 2]
-        f1, g1 = pair_maps[1, 0], pair_maps[1, 1]
-        across = matmul(f1, g0)
-        store_split(pair_split.at[0:128, 0:256], across)
-        store_split(pair_split.at[0:128, 256:512], g1)
-        store_split(pair_split.at[128:256, 0:256], g0 + matmul(b0, across))
-        store_split(pair_split.at[128:256, 256:512], matmul(b0, g1))
-
-    def z_prefix():
-        zmap_finish()
-        prefix_u[0] = jnp.where(eye_one, 1.0, 0.0)
-        prefix_u[1] = z_maps[0, 0]
-
-        def one(p, carry):
-            prefix_u[p + 1] = matmul(z_maps[p, 0], prefix_u[p])
-            return carry
-
-        lax.fori_loop(1, CHIPS_Z, one, 0)
-        x_maps[xs, 0] = prefix_u[CHIPS_Z]
-
-    def z_suffix():
-        suffix_v[CHIPS_Z, :, 0:128] = jnp.zeros((128, 128), F32)
-        suffix_v[CHIPS_Z, :, 128:256] = jnp.where(eye_one, 1.0, 0.0)
-
-        def one(i, carry):
-            p = CHIPS_Z - 1 - i
-            both = matmul(z_maps[p, 2], suffix_v[p + 1])
-            suffix_v[p, :, 0:128] = both[:, 0:128] + matmul(z_maps[p, 1], prefix_u[p])
-            suffix_v[p, :, 128:256] = both[:, 128:256]
-            return carry
-
-        lax.fori_loop(0, CHIPS_Z, one, 0)
-        x_maps[xs, 1] = suffix_v[0, :, 0:128]
-        x_maps[xs, 2] = suffix_v[0, :, 128:256]
-        xmap_start()
-
-    def z_splits():
-        def one(p, carry):
-            for j in range(3):
-                store_split(z_split.at[p, j], z_maps[p, j])
-            return carry
-
-        lax.fori_loop(0, CHIPS_Z, one, 0)
-        inner = core == 0
-        first = jnp.where(inner, z_maps[zs, 1], z_maps[zs, 0])
-        last = jnp.where(inner, z_maps[zs, 2], pair_maps[1, 2])
-        store_split(own_split.at[:, 0:256], first)
-        store_split(own_split.at[:, 256:512], last)
-        both = matmul(last, suffix_v[zs + 1])
-        store_split(last_split.at[:, 0:256], matmul(first, prefix_u[zs]) + both[:, 0:128])
-        store_split(last_split.at[:, 256:512], both[:, 128:256])
-
-    def x_splits():
-        xmap_finish()
-        for p in range(segs):
-            for j in range(3):
-                store_split(x_split.at[p, j], x_maps[p, j])
-
     def joined(a, b):
         a, b = split_twin(a).astype(BF16), split_twin(b).astype(BF16)
         return jnp.concatenate([a, a, b, b], axis=1)
 
-    def sweep(count, maps, box):
+    def sweep(count, maps, box, total):
         y = box[0, 0]
         enter_y[0] = jnp.zeros((8, 128), F32)
         lifted = [box[0, 1]]
         for p in range(1, count):
             enter_y[p] = y
-            lifted.append(box[p, 1] + times(y, maps[p, 1]))
-            y = box[p, 0] + times(y, maps[p, 0])
+            lifted.append(box[p, 1] + times(y, maps[p, 2]))
+            if total or p < count - 1:
+                y = box[p, 0] + times(y, maps[p, 0])
         x = lifted[count - 1]
         enter_x[count - 1] = jnp.zeros((8, 128), F32)
         for p in reversed(range(count - 1)):
             enter_x[p] = x
-            x = lifted[p] + times(x, maps[p, 2])
+            if total or p > 0:
+                x = lifted[p] + times(x, maps[p, 1])
         return y, x
 
     def chain_solve(piece):
@@ -701,15 +846,26 @@
         box_z[zs, 1] = behind
         z_start()
         z_finish()
-        y, x = sweep(CHIPS_Z, z_split, box_z)
+        y, x = sweep(CHIPS_Z, z_split, box_z, True)
         box_x[xs, 0] = y
         box_x[xs, 1] = x
         x_start()
-        base = jnp.where(core == 0, behind, ahead)
-        base = base + fold(dot_nt(joined(enter_y[zs], enter_x[zs]), own_split[...]))
+        y_in, x_in = enter_y[zs], enter_x[zs]
+        x_splits()
         x_finish()
-        sweep(segs, x_split, box_x)
-        return base + fold(dot_nt(joined(enter_y[xs], enter_x[xs]), last_split[...]))
+        sweep(segs, x_split, box_x, False)
+        y_far, x_far = enter_y[xs], enter_x[xs]
+        y_in = y_in + times(y_far, enter_split[0])
+        x_in = x_in + times(y_far, enter_split[1]) + times(x_far, enter_split[2])
+        both = fold(dot_nt(joined(y_in, x_in), pair_out[...]))
+        x_first, x_last = behind + both[:, 0:128], ahead + both[:, 128:256]
+        x_before = y_in + times(x_first, west_split[...])
+        inner = core == 0
+        return (
+            jnp.where(inner, x_first, x_last),
+            jnp.where(inner, x_before, x_first),
+            jnp.where(inner, x_last, x_in),
+        )
 
     def halves(pair):
         return jnp.concatenate([a.astype(BF16) for a in pair], axis=1)
@@ -728,15 +884,22 @@
         parts = [o[:, 128 * t : 128 * t + 128] for t in range(NT1)]
         return jnp.stack([jnp.where(upper(), parts[t], parts[t + 8]) for t in range(8)])
 
-    r_one, r2_one, x2_one = down(apply_one, inverse_one, right_one, (pair_products, pair_gains, None))
+    r_one, r2_one, x2_one = down(apply_one, inverse_one, right_one, (None, None, zmap_relay))
     right_two = restrict_one(r_one)
     r_two, r2_two, x2_two = down(apply_two, inverse_two, right_two, (z_prefix, z_suffix, z_splits))
-    piece = fold(dot_nt(halves(split_pair(r_two)), hot_two[...]))
-    x_splits()
-    answer = chain_solve(piece)
-    spread_two = pack_two(dot_nn(split_twin(answer).astype(BF16), hot_two[...]))
-    answer_two = up(apply_two, inverse_two, spread_two, r2_two, x2_two)
-    answer_one = up(apply_one, inverse_one, prolong_one(answer_two), r2_one, x2_one)
+    piece = fold(dot_nt(halves(split_pair(r_two)), hot_two[0]))
+    answers = chain_solve(piece)
+
+    def spread_two(p, answer):
+        return pack_two(dot_nn(split_twin(answer).astype(BF16), hot_two[p]))
+
+    spread = spread_two(0, answers[0])
+    put_two(0, spread)
+    for d, answer in enumerate((answers[1], answers[2], answers[0], answers[0])):
+        put_two(d + 1, jnp.where(exists(STEPS[d]), spread_two(d + 1, answer), 0.0))
+    answer_two = up(apply_two, inverse_two, spread, product_two(), r2_two, x2_two)
+    spread = prolong_one(answer_two)
+    answer_one = up(apply_one, inverse_one, spread, apply_one(3, spread), r2_one, x2_one)
     table[...] = answer_one
 
     def spread_rows(k, carry):
@@ -843,21 +1006,25 @@
                 pltpu.SMEM((3 * NT1,), jnp.int32),
                 pltpu.SMEM((3 * NT2,), jnp.int32),
                 pltpu.VMEM((256, 2048), BF16),
-                pltpu.VMEM((128, 256), BF16),
+                pltpu.VMEM((5, 128, 256), BF16),
                 pltpu.VMEM((6, 8, 8, 128), F32),
                 pltpu.VMEM((6, 8, 128), F32),
                 pltpu.VMEM((6, 4, 8, 8, 128), F32),
                 pltpu.VMEM((6, 4, 8, 128), F32),
                 pltpu.VMEM((CORES, 3, 128, 128), F32),
                 pltpu.VMEM((256, 512), BF16),
-                pltpu.VMEM((128, 512), BF16),
-                pltpu.VMEM((CHIPS_Z, 3, 128, 128), F32),
+                pltpu.VMEM((256, 512), BF16),
+                square,
+                pltpu.VMEM((128, 256), BF16),
+                pltpu.VMEM((4, 2, 128), jnp.int32),
+                pltpu.VMEM((CHIPS_Z, 384, 128), F32),
                 pltpu.VMEM((CHIPS_Z, 3, 128, 256), BF16),
                 pltpu.VMEM((CHIPS_Z + 1, 128, 128), F32),
-                pltpu.VMEM((CHIPS_Z + 1, 128, 256), F32),
+                pltpu.VMEM((CHIPS_Z + 1, 128, 128), F32),
+                pltpu.VMEM((CHIPS_Z + 1, 128, 128), F32),
                 pltpu.VMEM((segs, 3, 128, 128), F32),
                 pltpu.VMEM((segs, 3, 128, 256), BF16),
-                pltpu.VMEM((128, 512), BF16),
+                pltpu.VMEM((3, 128, 256), BF16),
                 pltpu.VMEM((CORES * narrow_size, 8, 128), F32),
                 pltpu.VMEM((CHIPS_Z, 2, 8, 128), F32),
                 pltpu.VMEM((segs, 2, 8, 128), F32),
@@ -872,12 +1039,18 @@
                 dma((6, 4)),
                 dma,
                 dma,
+                dma,
+                dma,
+                dma((4,)),
+                dma((4,)),
+                dma((CHIPS_Z,)),
+                dma((CHIPS_Z,)),
                 dma((CORES * narrow_size,)),
                 dma((CORES * narrow_size,)),
                 dma((CHIPS_Z,)),
                 dma((CHIPS_Z,)),
-                dma((segs,)),
-                dma((segs,)),
+                dma((2, segs)),
+                dma((2, segs)),
                 dma((CHIPS_Z,)),
                 dma((CHIPS_Z,)),
                 dma((segs,)),
@@ -893,8 +1066,8 @@
             north,
             fine_groups,
             tiles_one,
-            columns_one,
-            live_one,
+            columns_one.T,
+            live_one.T,
             coarse_groups.reshape(16, 128),
             tiles_two,
             columns_two,

time: 130 us -> 97.4 us (0.75)
  Pallas kernels: 125 us -> 95.5 us
  local copies, waits for them, and re-layouts: 4.37 us -> 1.67 us
    pallas_call x1, Pallas kernels: 125 us -> 95.5 us  [body(): pl.pallas_call(kernel_fn, out_shape=jax.ShapeDtypeStruct((COLS, GX, GY),...]
    unnamed x3 -> x1, local copies, waits for them, and re-layouts: 4.37 us -> 1.67 us
where the time goes in v2:
time: 97.4 us; the launch traced here: 97.2 us
  Pallas kernels  95.5 us (98%)
  local copies, waits for them, and re-layouts  1.67 us (2%)
    pallas_call x1, Pallas kernels, body(): pl.pallas_call(kernel_fn, out_shape=jax.ShapeDtypeStruct((COLS, GX, GY),...  95.5 us

profile of v2, /device:TPU:2, one launch (start us, length us, event | category | flops | bytes accessed | tf_op | source)
XLA Modules:
  0.0 97.2 jit_solution(5421028153715389696)
XLA Ops:
  0.0 95.5 %cycle.1 = f32[4,128,128]{2,1,0:T(8,128)} custom-call(f32[4,128,128]{2,1,0:T(8,128)} %refs_0_.1, f32[128,128]{1,0:T(8,128)} %refs_1_.1, f32[128,128]{1,0:T(8,128)} %refs_2_.1, s32[128,128]{1,0:T(8,128)} %refs_3_.1, f32[16,4,128,128]{3,2,1,0:T(8,128)} %refs_4_.1, s32[3,16]{1,0:T(4,128)} %bitcast.5, s32[3,16]{1,0:T(4,128)} %bitcast.6, s32[16,128]{1,0:T(8,128)} %bitcast.4, ...), custom_call_target="tpu_custom_call" | custom-call | tf_op jit(solution)/shard_map/cycle/pallas_call | solution.py:974
  95.5 1.7 %copy.17 = f32[4,128,128]{2,1,0:T(8,128)} copy(f32[4,128,128]{2,1,0:T(8,128)} %cycle.1) | data formatting | bytes 524288

commit v3 on v2

--- a/solution.py
+++ b/solution.py
@@ -91,17 +91,23 @@
     north,
     fine_groups,
     tiles_one,
-    columns_one,
-    live_one,
-    coarse_groups,
+    columns_one_in,
+    live_one_in,
+    coarse_groups_in,
     tiles_two,
-    columns_two,
-    live_two,
-    coarser_groups,
+    columns_two_in,
+    live_two_in,
+    coarser_groups_in,
     chain_forward,
     chain_gain,
     chain_backward,
     out,
+    columns_one,
+    live_one,
+    coarse_groups,
+    columns_two,
+    live_two,
+    coarser_groups,
     ext,
     groups_hi,
     groups_lo,
@@ -125,6 +131,9 @@
     segment,
     table,
     w_one,
+    w_far,
+    hot_fine,
+    groups_seg,
     w_two,
     picks_one,
     picks_two,
@@ -142,6 +151,7 @@
     west_map,
     west_split,
     group_box,
+    own_maps,
     z_maps,
     z_split,
     prefix_u,
@@ -168,6 +178,8 @@
     west_recv,
     group_send,
     group_recv,
+    ymap_send,
+    ymap_recv,
     relay_send,
     relay_recv,
     rhs_send,
@@ -206,12 +218,21 @@
         (fine_groups, groups_lo),
         (tiles_two, held_two),
         (tiles_one, held_one),
+        (columns_one_in, columns_one),
+        (live_one_in, live_one),
+        (coarse_groups_in, coarse_groups),
+        (columns_two_in, columns_two),
+        (live_two_in, live_two),
+        (coarser_groups_in, coarser_groups),
     )
     local = [pltpu.make_async_copy(a, b, local_sem.at[i]) for i, (a, b) in enumerate(loads)]
-    for c in local:
-        c.start()
-
     barrier = pltpu.get_barrier_semaphore()
+    for i in (4, 3, 5, 2, 6, 1, 7):
+        mate = (xs * seg_size + lax.rem(zs + i, CHIPS_Z) * CORES + core, q)
+        pl.semaphore_signal(barrier, inc=1, device_id=mate, device_id_type=MESH_ID)
+    for i in range(1, segs):
+        mate = (lax.rem(xs + i, segs) * seg_size + zs * CORES + core, q)
+        pl.semaphore_signal(barrier, inc=1, device_id=mate, device_id_type=MESH_ID)
     awaited = jnp.int32(0)
     for step in STEPS:
         there = exists(step)
@@ -226,13 +247,10 @@
     for i, j in group[1:]:
         mate = (w - core + lax.rem(core + i, CORES), lax.rem(q + j, narrow_size))
         pl.semaphore_signal(barrier, inc=1, device_id=mate, device_id_type=MESH_ID)
-    for i in range(1, CHIPS_Z):
-        mate = (xs * seg_size + lax.rem(zs + i, CHIPS_Z) * CORES + core, q)
-        pl.semaphore_signal(barrier, inc=1, device_id=mate, device_id_type=MESH_ID)
-    for i in range(1, segs):
-        mate = (lax.rem(xs + i, segs) * seg_size + zs * CORES + core, q)
-        pl.semaphore_signal(barrier, inc=1, device_id=mate, device_id_type=MESH_ID)
     awaited = awaited + len(group) - 1 + CHIPS_Z - 1 + segs - 1
+
+    for i in (0, 1, 2, 3, 4, 5, 14, 6, 9, 10, 11, 12, 13, 7, 8):
+        local[i].start()
 
     def fine_start(turn, source, arrays):
         lane = iota((8, 128), 1) // 4
@@ -337,6 +355,7 @@
 
     feeds_east = (core == CORES - 1) & (w < wide_size - 1)
     fed_from_west = (core == 0) & (w > 0)
+    local[14].wait()
     core_copy(core).start()
 
     @pl.when(feeds_east)
@@ -388,24 +407,36 @@
     x_start, x_finish = along(x_mate, segs, box_x, x_send, x_recv, xs)
     z_order = (1, 7, 2, 6, 3, 5, 4)
 
+    piece_rows = pl.ds(pl.multiple_of(192 * core + 48 * q, 16), 48)
+
     def zmap_copy(i, landing, mate):
-        half = pl.ds(pl.multiple_of(192 * core, 64), 192)
         return pltpu.make_async_remote_copy(
-            src_ref=z_maps.at[zs, half],
-            dst_ref=z_maps.at[landing, half],
+            src_ref=own_maps.at[piece_rows],
+            dst_ref=z_maps.at[landing, piece_rows],
             send_sem=zmap_send.at[i],
             recv_sem=zmap_recv.at[landing],
             device_id=mate,
             device_id_type=MESH_ID,
         )
 
-    def relay_copy(z, side):
+    def ymap_copy(i, other):
+        rows = pl.ds(pl.multiple_of(192 * core + 48 * other, 16), 48)
+        return pltpu.make_async_remote_copy(
+            src_ref=z_maps.at[:, rows],
+            dst_ref=z_maps.at[:, rows],
+            send_sem=ymap_send.at[i],
+            recv_sem=ymap_recv.at[other],
+            device_id=(w, lax.rem(q + i, narrow_size)),
+            device_id_type=MESH_ID,
+        )
+
+    def relay_copy(side):
         half = pl.ds(pl.multiple_of(192 * side, 64), 192)
         return pltpu.make_async_remote_copy(
-            src_ref=z_maps.at[z, half],
-            dst_ref=z_maps.at[z, half],
-            send_sem=relay_send.at[z],
-            recv_sem=relay_recv.at[z],
+            src_ref=z_maps.at[:, half],
+            dst_ref=z_maps.at[:, half],
+            send_sem=relay_send,
+            recv_sem=relay_recv,
             device_id=(w - core + (1 - core), q),
             device_id_type=MESH_ID,
         )
@@ -416,9 +447,10 @@
         f0, b0 = pair_maps[0, 0], pair_maps[0, 2]
         f1, b1 = pair_maps[1, 0], pair_maps[1, 2]
         both = matmul(f1, f0)
-        z_maps[zs, 0:128] = both
-        z_maps[zs, 128:256] = matmul(b0, b1)
-        z_maps[zs, 256:384] = f0 + matmul(b0, both)
+        own_maps[0:128] = both
+        own_maps[128:256] = matmul(b0, b1)
+        own_maps[256:384] = f0 + matmul(b0, both)
+        z_maps[zs, piece_rows] = own_maps[piece_rows]
         for i in z_order:
             _, mate = z_mate(i)
             zmap_copy(i, zs, mate).start()
@@ -432,11 +464,19 @@
         store_split(pair_split.at[128:256, 0:256], g0 + matmul(b0, across))
         store_split(pair_split.at[128:256, 256:512], matmul(b0, g1))
 
-    def zmap_relay():
+    def zmap_across():
         for i in z_order:
             other, mate = z_mate(i)
             zmap_copy(i, other, mate).wait_recv()
-            relay_copy(other, core).start()
+            zmap_copy(i, zs, mate).wait_send()
+        for i in range(1, narrow_size):
+            ymap_copy(i, q).start()
+
+    def zmap_relay():
+        for i in range(1, narrow_size):
+            ymap_copy(i, lax.rem(q + i, narrow_size)).wait_recv()
+            ymap_copy(i, q).wait_send()
+        relay_copy(core).start()
 
     def times_map(split_map, m):
         hi = m.astype(BF16)
@@ -445,11 +485,8 @@
         return dot_nn(lhs, jnp.concatenate([hi, hi, lo], axis=0))
 
     def z_prefix():
-        for i in z_order:
-            other, mate = z_mate(i)
-            zmap_copy(i, zs, mate).wait_send()
-            relay_copy(other, 1 - core).wait_recv()
-            relay_copy(other, core).wait_send()
+        relay_copy(1 - core).wait_recv()
+        relay_copy(core).wait_send()
 
         def split_one(p, carry):
             for j in range(3):
@@ -505,6 +542,10 @@
                 def _():
                     xmap_copy(part, i, xs, mate).start()
 
+    def z_composites():
+        z_prefix()
+        z_suffix()
+
     def z_splits():
         store_split(enter_split.at[0], prefix_u[zs])
         store_split(enter_split.at[1], suffix_v[zs + 1])
@@ -554,6 +595,14 @@
     groups = groups_lo[...]
     groups_hi[...] = groups // 128
     groups_lo[...] = lax.rem(groups, 128)
+    groups_seg[...] = groups // 256
+    turned = jnp.transpose(lax.rem(groups, 256).astype(F32))
+    wide_lane = iota((GY, 256), 1).astype(F32)
+    for i in range(GX):
+        hot = turned[:, i : i + 1] == wide_lane
+        hot_fine[GY * i : GY * i + GY, :] = jnp.where(hot, 1.0, 0.0).astype(BF16)
+    for i in range(9, 14):
+        local[i].wait()
     for r in range(NT1):
         for k in range(3):
             spots_one[3 * r + k] = jnp.where(live_one[k, r] == 1, columns_one[k, r], 5 * NT1)
@@ -602,7 +651,12 @@
                 m = held_one[r, k]
                 if k == 0:
                     diags.append(jnp.sum(jnp.where(eye_one, m, 0.0), axis=0, keepdims=True))
-                store_split(w_one.at[r, :, pl.ds(256 * k, 256)], m)
+                    store_split(w_one.at[r], m)
+                else:
+                    m = jnp.transpose(m)
+                    hi = m.astype(BF16)
+                    w_far[r, 256 * k - 256 : 256 * k - 128, :] = hi
+                    w_far[r, 256 * k - 128 : 256 * k, :] = (m - hi.astype(F32)).astype(BF16)
         low, high = (jnp.broadcast_to(d, (8, 128)) for d in diags)
         table[t] = 1.0 / jnp.where(upper(), low, high)
         return carry
@@ -669,29 +723,30 @@
                 high_rows[pl.ds(8 * i + 4 * h + c, 8, stride=8), :] = hi
                 low_rows[pl.ds(8 * i + 4 * h + c, 8, stride=8), :] = lo
 
-    segment[...] = jnp.zeros((128, 128), F32)
-    half = jnp.where(upper(), 0, 8)
-    tall = iota((128, 128), 0)
-    chunk = 8
+    segment[...] = jnp.zeros((64, 256), F32)
+    half = jnp.where(upper(), 0, 4)
+    chunk = 16
 
     def gather_up(step, carry):
-        lhs, rhs = [], []
+        lhs = []
         for j in range(chunk):
             i = step * chunk + j
-            hi_index = jnp.broadcast_to(groups_hi[pl.ds(i, 1), :], (8, 128))
-            lo_index = groups_lo[pl.ds(i, 1), :]
+            index = jnp.broadcast_to(groups_seg[pl.ds(i, 1), :], (8, 128))
             at = pl.multiple_of(8 * i, 8)
             v_hi = high_rows[pl.ds(at, 8), :]
             v_lo = low_rows[pl.ds(at, 8), :]
-            masks = [hi_index == half + t for t in range(8)]
+            masks = [index == half + t for t in range(4)]
             rows = [jnp.where(m, v_hi, 0.0) for m in masks] + [jnp.where(m, v_lo, 0.0) for m in masks]
             lhs.append(jnp.concatenate(rows, axis=0).astype(BF16))
-            rhs.append(jnp.where(tall == lo_index, 1.0, 0.0).astype(BF16))
-        segment[...] += dot_nt(jnp.concatenate(lhs, axis=1), jnp.concatenate(rhs, axis=1))
+        span = pl.ds(pl.multiple_of(step * (chunk * GY), chunk * GY), chunk * GY)
+        segment[...] += dot_nn(jnp.concatenate(lhs, axis=1), hot_fine[span, :])
         return carry
 
     lax.fori_loop(0, GX // chunk, gather_up, 0)
-    right_one = (segment[0:64, :] + segment[64:128, :]).reshape(8, 8, 128)
+    folded = segment[0:32, :] + segment[32:64, :]
+    right_one = jnp.stack(
+        [folded[8 * (t // 2) : 8 * (t // 2) + 8, 128 * (t % 2) : 128 * (t % 2) + 128] for t in range(8)]
+    )
 
     def coarse_copy(sent, box, sends, receives, k, d, landing):
         return pltpu.make_async_remote_copy(
@@ -734,7 +789,7 @@
         own = []
         for r in range(NT1):
             a = picks_one[r].astype(BF16)
-            own.append(dot_nt(jnp.concatenate([a, a], axis=1), w_one[r, :, 0:256]))
+            own.append(dot_nt(jnp.concatenate([a, a], axis=1), w_one[r]))
         own = [jnp.where(upper(), fold(own[t]), fold(own[t + 8])) for t in range(8)]
         if meanwhile is not None:
             meanwhile()
@@ -749,7 +804,7 @@
             for j in range(3):
                 a = picks_one[spots_one[3 * r + j]].astype(BF16)
                 parts += [a, a]
-            outs.append(dot_nt(jnp.concatenate(parts, axis=1), w_one[r, :, 256:1024]))
+            outs.append(dot_nn(jnp.concatenate(parts, axis=1), w_far[r]))
         return jnp.stack(
             [own[t] + jnp.where(upper(), fold(outs[t]), fold(outs[t + 8])) for t in range(8)]
         )
@@ -830,6 +885,7 @@
 
         for i, j in group[1:]:
             rhs_copy(i, j, slot).start()
+        z_splits()
         for i, j in group[1:]:
             other = lax.rem(core + i, CORES) * narrow_size + lax.rem(q + j, narrow_size)
             rhs_copy(i, j, other).wait_recv()
@@ -884,9 +940,9 @@
         parts = [o[:, 128 * t : 128 * t + 128] for t in range(NT1)]
         return jnp.stack([jnp.where(upper(), parts[t], parts[t + 8]) for t in range(8)])
 
-    r_one, r2_one, x2_one = down(apply_one, inverse_one, right_one, (None, None, zmap_relay))
+    r_one, r2_one, x2_one = down(apply_one, inverse_one, right_one, (zmap_across, None, None))
     right_two = restrict_one(r_one)
-    r_two, r2_two, x2_two = down(apply_two, inverse_two, right_two, (z_prefix, z_suffix, z_splits))
+    r_two, r2_two, x2_two = down(apply_two, inverse_two, right_two, (zmap_relay, z_composites, None))
     piece = fold(dot_nt(halves(split_pair(r_two)), hot_two[0]))
     answers = chain_solve(piece)
 
@@ -916,7 +972,7 @@
             field_a[c, pl.ds(pl.multiple_of(TOP + at, 8), 8), 0:128] = total
         return carry
 
-    lax.fori_loop(0, GX // 8, spread_rows, 0)
+    lax.fori_loop(0, GX // 8, spread_rows, 0, unroll=4)
     fine_start(1, field_a, 4)
     fine_send_all(1, 4)
     fine_wait(1, 4)
@@ -961,7 +1017,6 @@
     ):
         hbm = pl.BlockSpec(memory_space=pl.ANY)
         vmem = pl.BlockSpec(memory_space=pltpu.VMEM)
-        smem = pl.BlockSpec(memory_space=pltpu.SMEM)
         dma = pltpu.SemaphoreType.DMA
         big = pltpu.VMEM((COLS, EXT_ROWS, EXT_LANES), F32)
         weight = pltpu.VMEM((EXT_ROWS - 16, EXT_LANES), F32)
@@ -974,9 +1029,15 @@
         return pl.pallas_call(
             kernel_fn,
             out_shape=jax.ShapeDtypeStruct((COLS, GX, GY), F32),
-            in_specs=[hbm] * 5 + [smem] * 2 + [vmem, hbm] + [smem] * 2 + [vmem] + [hbm] * 3,
+            in_specs=[hbm] * 15,
             out_specs=vmem,
             scratch_shapes=[
+                pltpu.SMEM((3, NT1), jnp.int32),
+                pltpu.SMEM((3, NT1), jnp.int32),
+                pltpu.VMEM((16, 128), jnp.int32),
+                pltpu.SMEM((NT2, 3), jnp.int32),
+                pltpu.SMEM((NT2, 3), jnp.int32),
+                pltpu.VMEM((2, 128), jnp.int32),
                 pltpu.VMEM((6, EXT_ROWS, EXT_LANES), F32),
                 indices,
                 indices,
@@ -997,9 +1058,12 @@
                 pltpu.VMEM((COLS, GX, GY), F32),
                 pltpu.VMEM((8 * GX, GY), F32),
                 pltpu.VMEM((8 * GX, GY), F32),
-                square,
+                pltpu.VMEM((64, 256), F32),
                 pltpu.VMEM((8, 8, 128), F32),
-                pltpu.VMEM((NT1, 128, 1024), BF16),
+                pltpu.VMEM((NT1, 128, 256), BF16),
+                pltpu.VMEM((NT1, 768, 128), BF16),
+                pltpu.VMEM((GX * GY, 256), BF16),
+                indices,
                 pltpu.VMEM((NT2, 128, 512), BF16),
                 pltpu.VMEM((5 * NT1 + 1, 8, 128), F32),
                 pltpu.VMEM((5 * NT2 + 1, 8, 128), F32),
@@ -1017,6 +1081,7 @@
                 square,
                 pltpu.VMEM((128, 256), BF16),
                 pltpu.VMEM((4, 2, 128), jnp.int32),
+                pltpu.VMEM((384, 128), F32),
                 pltpu.VMEM((CHIPS_Z, 384, 128), F32),
                 pltpu.VMEM((CHIPS_Z, 3, 128, 256), BF16),
                 pltpu.VMEM((CHIPS_Z + 1, 128, 128), F32),
@@ -1030,7 +1095,7 @@
                 pltpu.VMEM((segs, 2, 8, 128), F32),
                 pltpu.VMEM((CHIPS_Z, 8, 128), F32),
                 pltpu.VMEM((CHIPS_Z, 8, 128), F32),
-                dma((9,)),
+                dma((15,)),
                 dma((2, 8)),
                 dma((2, 8)),
                 dma((6, 4)),
@@ -1043,8 +1108,10 @@
                 dma,
                 dma((4,)),
                 dma((4,)),
-                dma((CHIPS_Z,)),
-                dma((CHIPS_Z,)),
+                dma((narrow_size,)),
+                dma((narrow_size,)),
+                dma,
+                dma,
                 dma((CORES * narrow_size,)),
                 dma((CORES * narrow_size,)),
                 dma((CHIPS_Z,)),

time: 97.4 us -> 90.7 us (0.931)
  Pallas kernels: 95.5 us -> 88.9 us
    pallas_call x1, Pallas kernels: 95.5 us -> 88.9 us  [body(): pl.pallas_call(kernel_fn, out_shape=jax.ShapeDtypeStruct((COLS, GX, GY),...]
where the time goes in v3:
time: 90.7 us; the launch traced here: 90.6 us
  Pallas kernels  88.9 us (98%)
  local copies, waits for them, and re-layouts  1.67 us (2%)
    pallas_call x1, Pallas kernels, body(): pl.pallas_call(kernel_fn, out_shape=jax.ShapeDtypeStruct((COLS, GX, GY),...  88.9 us

profile of v3, /device:TPU:2, one launch (start us, length us, event | category | flops | bytes accessed | tf_op | source)
XLA Modules:
  0.0 90.6 jit_solution(9209714248608441481)
XLA Ops:
  0.0 88.9 %cycle.1 = f32[4,128,128]{2,1,0:T(8,128)} custom-call(f32[4,128,128]{2,1,0:T(8,128)} %refs_0_.1, f32[128,128]{1,0:T(8,128)} %refs_1_.1, f32[128,128]{1,0:T(8,128)} %refs_2_.1, s32[128,128]{1,0:T(8,128)} %refs_3_.1, f32[16,4,128,128]{3,2,1,0:T(8,128)} %refs_4_.1, s32[3,16]{1,0:T(4,128)} %bitcast.5, s32[3,16]{1,0:T(4,128)} %bitcast.6, s32[16,128]{1,0:T(8,128)} %bitcast.4, ...), custom_call_target="tpu_custom_call" | custom-call | tf_op jit(solution)/shard_map/cycle/pallas_call | solution.py:1029
  88.9 1.7 %copy.17 = f32[4,128,128]{2,1,0:T(8,128)} copy(f32[4,128,128]{2,1,0:T(8,128)} %cycle.1) | data formatting | bytes 524288

commit v4 on v3

--- a/solution.py
+++ b/solution.py
@@ -419,13 +419,13 @@
             device_id_type=MESH_ID,
         )
 
-    def ymap_copy(i, other):
+    def ymap_copy(i, z, other):
         rows = pl.ds(pl.multiple_of(192 * core + 48 * other, 16), 48)
         return pltpu.make_async_remote_copy(
-            src_ref=z_maps.at[:, rows],
-            dst_ref=z_maps.at[:, rows],
-            send_sem=ymap_send.at[i],
-            recv_sem=ymap_recv.at[other],
+            src_ref=z_maps.at[z, rows],
+            dst_ref=z_maps.at[z, rows],
+            send_sem=ymap_send.at[i, z],
+            recv_sem=ymap_recv.at[other, z],
             device_id=(w, lax.rem(q + i, narrow_size)),
             device_id_type=MESH_ID,
         )
@@ -464,18 +464,29 @@
         store_split(pair_split.at[128:256, 0:256], g0 + matmul(b0, across))
         store_split(pair_split.at[128:256, 256:512], matmul(b0, g1))
 
-    def zmap_across():
-        for i in z_order:
+    def ymap_start(z):
+        for i in range(1, narrow_size):
+            ymap_copy(i, z, q).start()
+
+    def zmap_take(order):
+        for i in order:
             other, mate = z_mate(i)
             zmap_copy(i, other, mate).wait_recv()
             zmap_copy(i, zs, mate).wait_send()
-        for i in range(1, narrow_size):
-            ymap_copy(i, q).start()
+            ymap_start(other)
+
+    def zmap_near():
+        ymap_start(zs)
+        zmap_take(z_order[:4])
+
+    def zmap_far():
+        zmap_take(z_order[4:])
 
     def zmap_relay():
         for i in range(1, narrow_size):
-            ymap_copy(i, lax.rem(q + i, narrow_size)).wait_recv()
-            ymap_copy(i, q).wait_send()
+            for z in range(CHIPS_Z):
+                ymap_copy(i, z, lax.rem(q + i, narrow_size)).wait_recv()
+                ymap_copy(i, z, q).wait_send()
         relay_copy(core).start()
 
     def times_map(split_map, m):
@@ -509,18 +520,21 @@
         x_maps[xs, 1] = suffix_w[0]
 
     def xmap_copy(part, i, landing, mate):
-        span = pl.ds(0, 2) if part == 0 else pl.ds(2, 1)
         return pltpu.make_async_remote_copy(
-            src_ref=x_maps.at[xs, span],
-            dst_ref=x_maps.at[landing, span],
+            src_ref=x_maps.at[xs, part],
+            dst_ref=x_maps.at[landing, part],
             send_sem=xmap_send.at[part, i],
             recv_sem=xmap_recv.at[part, landing],
             device_id=mate,
             device_id_type=MESH_ID,
         )
 
-    def has_map(part, x):
-        return (x > 0) & (x < segs - 1) if part == 0 else x > 0
+    def has_map(part, source, target):
+        if part == 0:
+            return (source > 0) & (source < segs - 1)
+        if part == 1:
+            return (source < segs - 1) & (target < source)
+        return target < source
 
     def z_suffix():
         suffix_v[CHIPS_Z] = jnp.zeros((128, 128), F32)
@@ -534,11 +548,11 @@
 
         lax.fori_loop(0, CHIPS_Z, one, 0)
         x_maps[xs, 2] = suffix_v[0]
-        for part in range(2):
+        for part in range(3):
             for i in range(1, segs):
-                _, mate = x_mate(i)
-
-                @pl.when(has_map(part, xs))
+                other, mate = x_mate(i)
+
+                @pl.when(has_map(part, xs, other))
                 def _():
                     xmap_copy(part, i, xs, mate).start()
 
@@ -574,15 +588,15 @@
             mark_two(d + 1, group_box[d], q + STEPS[d][1])
 
     def x_splits():
-        for part in range(2):
+        for part in range(3):
             for i in range(1, segs):
                 other, mate = x_mate(i)
 
-                @pl.when(has_map(part, other))
+                @pl.when(has_map(part, other, xs))
                 def _():
                     xmap_copy(part, i, other, mate).wait_recv()
 
-                @pl.when(has_map(part, xs))
+                @pl.when(has_map(part, xs, other))
                 def _():
                     xmap_copy(part, i, xs, mate).wait_send()
 
@@ -940,7 +954,7 @@
         parts = [o[:, 128 * t : 128 * t + 128] for t in range(NT1)]
         return jnp.stack([jnp.where(upper(), parts[t], parts[t + 8]) for t in range(8)])
 
-    r_one, r2_one, x2_one = down(apply_one, inverse_one, right_one, (zmap_across, None, None))
+    r_one, r2_one, x2_one = down(apply_one, inverse_one, right_one, (zmap_near, zmap_far, None))
     right_two = restrict_one(r_one)
     r_two, r2_two, x2_two = down(apply_two, inverse_two, right_two, (zmap_relay, z_composites, None))
     piece = fold(dot_nt(halves(split_pair(r_two)), hot_two[0]))
@@ -1028,7 +1042,7 @@
 
         return pl.pallas_call(
             kernel_fn,
-            out_shape=jax.ShapeDtypeStruct((COLS, GX, GY), F32),
+            out_shape=pltpu.VMEM((COLS, GX, GY), F32),
             in_specs=[hbm] * 15,
             out_specs=vmem,
             scratch_shapes=[
@@ -1108,16 +1122,16 @@
                 dma,
                 dma((4,)),
                 dma((4,)),
-                dma((narrow_size,)),
-                dma((narrow_size,)),
+                dma((narrow_size, CHIPS_Z)),
+                dma((narrow_size, CHIPS_Z)),
                 dma,
                 dma,
                 dma((CORES * narrow_size,)),
                 dma((CORES * narrow_size,)),
                 dma((CHIPS_Z,)),
                 dma((CHIPS_Z,)),
-                dma((2, segs)),
-                dma((2, segs)),
+                dma((3, segs)),
+                dma((3, segs)),
                 dma((CHIPS_Z,)),
                 dma((CHIPS_Z,)),
                 dma((segs,)),

time: 90.7 us -> 87 us (0.959)
  Pallas kernels: 88.9 us -> 86 us
  local copies, waits for them, and re-layouts: 1.67 us -> 0.71 us
    pallas_call x1, Pallas kernels: 88.9 us -> 86 us  [body(): pl.pallas_call(kernel_fn, out_shape=pltpu.VMEM((COLS, GX, GY), F32), in_s...]
    unnamed x1, local copies, waits for them, and re-layouts: 1.67 us -> 0.71 us
where the time goes in v4:
time: 87 us; the launch traced here: 86.8 us
  Pallas kernels  86 us (99%)
    pallas_call x1, Pallas kernels, body(): pl.pallas_call(kernel_fn, out_shape=pltpu.VMEM((COLS, GX, GY), F32), in_s...  86 us

profile of v4, /device:TPU:2, one launch (start us, length us, event | category | flops | bytes accessed | tf_op | source)
XLA Modules:
  0.0 86.8 jit_solution(1316165866972218950)
XLA Ops:
  0.0 86.0 %cycle.1 = f32[4,128,128]{2,1,0:T(8,128)S(1)} custom-call(f32[4,128,128]{2,1,0:T(8,128)} %refs_0_.1, f32[128,128]{1,0:T(8,128)} %refs_1_.1, f32[128,128]{1,0:T(8,128)} %refs_2_.1, s32[128,128]{1,0:T(8,128)} %refs_3_.1, f32[16,4,128,128]{3,2,1,0:T(8,128)} %refs_4_.1, s32[3,16]{1,0:T(4,128)} %bitcast.5, s32[3,16]{1,0:T(4,128)} %bitcast.6, s32[16,128]{1,0:T(8,128)} %bitcast.4, ...), custom_call_target="tpu_custom_call" | custom-call | tf_op jit(solution)/shard_map/cycle/pallas_call | solution.py:1043
  86.1 0.7 copy.17

commit v5 on v4

--- a/solution.py
+++ b/solution.py
@@ -669,8 +669,8 @@
                 else:
                     m = jnp.transpose(m)
                     hi = m.astype(BF16)
-                    w_far[r, 256 * k - 256 : 256 * k - 128, :] = hi
-                    w_far[r, 256 * k - 128 : 256 * k, :] = (m - hi.astype(F32)).astype(BF16)
+                    w_far[r, 128 * k - 128 : 128 * k, 0:128] = hi
+                    w_far[r, 128 * k - 128 : 128 * k, 128:256] = (m - hi.astype(F32)).astype(BF16)
         low, high = (jnp.broadcast_to(d, (8, 128)) for d in diags)
         table[t] = 1.0 / jnp.where(upper(), low, high)
         return carry
@@ -756,7 +756,7 @@
         segment[...] += dot_nn(jnp.concatenate(lhs, axis=1), hot_fine[span, :])
         return carry
 
-    lax.fori_loop(0, GX // chunk, gather_up, 0)
+    lax.fori_loop(0, GX // chunk, gather_up, 0, unroll=4)
     folded = segment[0:32, :] + segment[32:64, :]
     right_one = jnp.stack(
         [folded[8 * (t // 2) : 8 * (t // 2) + 8, 128 * (t % 2) : 128 * (t % 2) + 128] for t in range(8)]
@@ -816,9 +816,9 @@
         for r in range(NT1):
             parts = []
             for j in range(3):
-                a = picks_one[spots_one[3 * r + j]].astype(BF16)
-                parts += [a, a]
-            outs.append(dot_nn(jnp.concatenate(parts, axis=1), w_far[r]))
+                parts.append(picks_one[spots_one[3 * r + j]].astype(BF16))
+            both = dot_nn(jnp.concatenate(parts, axis=1), w_far[r])
+            outs.append(both[:, 0:128] + both[:, 128:256])
         return jnp.stack(
             [own[t] + jnp.where(upper(), fold(outs[t]), fold(outs[t + 8])) for t in range(8)]
         )
@@ -1075,7 +1075,7 @@
                 pltpu.VMEM((64, 256), F32),
                 pltpu.VMEM((8, 8, 128), F32),
                 pltpu.VMEM((NT1, 128, 256), BF16),
-                pltpu.VMEM((NT1, 768, 128), BF16),
+                pltpu.VMEM((NT1, 384, 256), BF16),
                 pltpu.VMEM((GX * GY, 256), BF16),
                 indices,
                 pltpu.VMEM((NT2, 128, 512), BF16),

time: 87 us -> 86.2 us (level)
  no operation moved by 1% of the time
where the time goes in v5:
time: 86.2 us; the launch traced here: 86 us
  Pallas kernels  85.3 us (99%)
    pallas_call x1, Pallas kernels, body(): pl.pallas_call(kernel_fn, out_shape=pltpu.VMEM((COLS, GX, GY), F32), in_s...  85.3 us

profile of v5, /device:TPU:2, one launch (start us, length us, event | category | flops | bytes accessed | tf_op | source)
XLA Modules:
  0.0 86.0 jit_solution(3771624304277156917)
XLA Ops:
  0.0 85.3 %cycle.1 = f32[4,128,128]{2,1,0:T(8,128)S(1)} custom-call(f32[4,128,128]{2,1,0:T(8,128)} %refs_0_.1, f32[128,128]{1,0:T(8,128)} %refs_1_.1, f32[128,128]{1,0:T(8,128)} %refs_2_.1, s32[128,128]{1,0:T(8,128)} %refs_3_.1, f32[16,4,128,128]{3,2,1,0:T(8,128)} %refs_4_.1, s32[3,16]{1,0:T(4,128)} %bitcast.5, s32[3,16]{1,0:T(4,128)} %bitcast.6, s32[16,128]{1,0:T(8,128)} %bitcast.4, ...), custom_call_target="tpu_custom_call" | custom-call | tf_op jit(solution)/shard_map/cycle/pallas_call | solution.py:1043
  85.3 0.7 copy.17
